TPU v7x, 256 devices: a whole 4x4x8 slice. The times are simulated.
256 devices in a mesh: gx: 8 (over x, y_lo), gy: 32 (over y_hi, z, core).
Axes of the slice: x: 4, y: 4 (y_hi: 2, y_lo: 2; y = y_hi * 2 + y_lo), z: 8, core: 2. Of those that a mesh axis runs over, the one named last changes fastest.
Arguments:
- fields: bfloat16 [64, 512, 1024], P('gx', 'gy'), may hold values from -6 to 6
- grad_out: bfloat16 [64, 512, 1024], P('gx', 'gy'), may hold values from -6 to 6
- norm_gain: float32 [1024], replicated, may hold values from 0.25 to 1.75
- w_qkv: bfloat16 [1024, 3072], replicated, may hold values from -3 to 3
- brick_mask: int32 [8, 64, 8], P('gx', 'gy'), may hold values 0 or 1
Outputs:
- output: bfloat16 [64, 512, 1024], P('gx', 'gy')
- grad_in: bfloat16 [64, 512, 1024], P('gx', 'gy')
- w_grad_qkv: float32 [1024, 3072], P(('gx', 'gy'))
- gain_grad: float32 [1024], P(('gx', 'gy'))
All inputs are finite; a program needn't handle non-finite values. No bound on the sum of `brick_mask` on one device may be relied on, other than what follows from the above.
Results may differ from a plain program's by a relative error of at most 0.017.
The roundings to bfloat16 on the way count: a program that leaves them out, or rounds other values in their place, can miss the bound.
Values may be sent and summed in bfloat16 or wider, within the bound.
A program may use at most 128 MiB of HBM per device.

v0:
```python
import jax
import jax.numpy as jnp
from jax import lax
from jax.sharding import PartitionSpec as P

HEADS = 16
BRICK = 8


EPSILON = 1e-05
NEG_BIG = -1e30


def padded(value, sides, width):
    for axis, dim in sides:
        peers, length = (lax.axis_size(axis), value.shape[dim])
        up = [(i, (i + 1) % peers) for i in range(peers)]
        down = [(j, i) for i, j in up]
        last = lax.slice_in_dim(value, length - width, length, axis=dim)
        first = lax.slice_in_dim(value, 0, width, axis=dim)
        before = lax.ppermute(last, axis, up)
        after = lax.ppermute(first, axis, down)
        value = jnp.concatenate([before, value, after], axis=dim)
    return value


def to_bricks(table):
    tile_rows, tile_cols, channels = table.shape
    shaped = table.reshape(tile_rows // BRICK, BRICK, tile_cols // BRICK, BRICK, channels)
    return shaped.transpose(0, 2, 1, 3, 4).reshape(
        tile_rows // BRICK, tile_cols // BRICK, BRICK * BRICK, channels
    )


def from_bricks(blocks):
    b_rows, b_cols, inside, channels = blocks.shape
    shaped = blocks.reshape(b_rows, b_cols, BRICK, BRICK, channels)
    return shaped.transpose(0, 2, 1, 3, 4).reshape(b_rows * BRICK, b_cols * BRICK, channels)


def windows(extended, tile_rows, tile_cols):
    pieces = []
    for row_step in range(3):
        for col_step in range(3):
            pieces.append(
                to_bricks(
                    extended[
                        BRICK * row_step : BRICK * row_step + tile_rows,
                        BRICK * col_step : BRICK * col_step + tile_cols,
                    ]
                )
            )
    stacked = jnp.stack(pieces, axis=2)
    return stacked.reshape(stacked.shape[0], stacked.shape[1], 9 * BRICK * BRICK, stacked.shape[-1])


def allowed_keys(mask_tile):
    ones_col = jnp.ones(mask_tile.shape[:2] + (1,), jnp.int32)
    all_nine = jnp.concatenate([mask_tile[:, :, :4], ones_col, mask_tile[:, :, 4:]], axis=2)
    spread = jnp.broadcast_to(all_nine[:, :, :, None], all_nine.shape + (BRICK * BRICK,))
    return spread.reshape(all_nine.shape[0], all_nine.shape[1], 9 * BRICK * BRICK) > 0


def spread_bricks(grad_nb):
    total = None
    for row_step in range(3):
        for col_step in range(3):
            piece = jnp.pad(
                grad_nb[:, :, 3 * row_step + col_step],
                ((row_step, 2 - row_step), (col_step, 2 - col_step), (0, 0), (0, 0)),
            )
            total = piece if total is None else total + piece
    return total


def attend_both(q_tile, ext_tile, grad_tile, mask_tile):
    tile_rows, tile_cols, feat_width = q_tile.shape
    head_dim = feat_width // HEADS
    scale_qk = head_dim ** (-0.5)
    q_bricks = to_bricks(q_tile)
    b_rows, b_cols = (q_bricks.shape[0], q_bricks.shape[1])
    inside = BRICK * BRICK
    head_q = q_bricks.reshape(b_rows, b_cols, inside, HEADS, head_dim)
    key_win = windows(ext_tile, tile_rows, tile_cols)
    head_k = key_win[..., :feat_width].reshape(b_rows, b_cols, 9 * inside, HEADS, head_dim)
    head_v = key_win[..., feat_width:].reshape(b_rows, b_cols, 9 * inside, HEADS, head_dim)
    scores = (
        jnp.einsum("abqhd,abkhd->abhqk", head_q, head_k, preferred_element_type=jnp.float32)
        * scale_qk
    )
    allowed = allowed_keys(mask_tile)
    scores = jnp.where(allowed[:, :, None, None, :], scores, NEG_BIG)
    row_max = jnp.max(scores, axis=-1, keepdims=True)
    exp_s = jnp.exp(scores - row_max)
    prob_f = exp_s / jnp.sum(exp_s, axis=-1, keepdims=True)
    weights = prob_f.astype(jnp.bfloat16)
    mixed_f = jnp.einsum("abhqk,abkhd->abqhd", weights, head_v, preferred_element_type=jnp.float32)
    mixed_b = mixed_f.astype(jnp.bfloat16).reshape(b_rows, b_cols, inside, feat_width)
    grad_head = to_bricks(grad_tile).reshape(b_rows, b_cols, inside, HEADS, head_dim)
    grad_prob = jnp.einsum(
        "abqhd,abkhd->abhqk", grad_head, head_v, preferred_element_type=jnp.float32
    )
    inner_sum = jnp.sum(prob_f * grad_prob, axis=-1, keepdims=True)
    grad_score = (prob_f * (grad_prob - inner_sum) * scale_qk).astype(jnp.bfloat16)
    grad_q = jnp.einsum(
        "abhqk,abkhd->abqhd", grad_score, head_k, preferred_element_type=jnp.float32
    ).astype(jnp.bfloat16)
    grad_k = jnp.einsum(
        "abhqk,abqhd->abkhd", grad_score, head_q, preferred_element_type=jnp.float32
    )
    grad_v = jnp.einsum(
        "abhqk,abqhd->abkhd", weights, grad_head, preferred_element_type=jnp.float32
    )
    grad_k = grad_k.reshape(b_rows, b_cols, 9, inside, feat_width)
    grad_v = grad_v.reshape(b_rows, b_cols, 9, inside, feat_width)
    grad_q = grad_q.reshape(b_rows, b_cols, inside, feat_width)
    return (from_bricks(mixed_b), from_bricks(grad_q), grad_k, grad_v)


def per_device(fields, grad_out, norm_gain, w_qkv, brick_mask):
    tile_rows, tile_cols, feat_width = fields.shape
    tok_count = tile_rows * tile_cols
    flat_in = fields.reshape(tok_count, feat_width).astype(jnp.float32)
    inv_rms = lax.rsqrt(jnp.mean(flat_in * flat_in, axis=1, keepdims=True) + EPSILON)
    normed = (flat_in * inv_rms * norm_gain).astype(jnp.bfloat16)
    proj_all = jnp.dot(normed, w_qkv, preferred_element_type=jnp.float32).astype(jnp.bfloat16)
    queries = proj_all[:, :feat_width].reshape(tile_rows, tile_cols, feat_width)
    keyval = proj_all[:, feat_width:].reshape(tile_rows, tile_cols, 2 * feat_width)
    extended = padded(keyval, (("gx", 0), ("gy", 1)), BRICK)
    grad_flat = grad_out.reshape(tok_count, feat_width)
    mixed_r, grad_q_r, grad_k_r, grad_v_r = attend_both(queries, extended, grad_out, brick_mask)
    key_bricks = spread_bricks(grad_k_r)
    value_bricks = spread_bricks(grad_v_r)
    ext_grad = from_bricks(jnp.concatenate([key_bricks, value_bricks], axis=-1))
    attn_flat = mixed_r.reshape(tok_count, feat_width)
    output = (flat_in + attn_flat.astype(jnp.float32)).astype(jnp.bfloat16).reshape(fields.shape)
    cols_pack = jnp.concatenate([ext_grad[:, :BRICK], ext_grad[:, -BRICK:]], axis=1)
    cols_back = padded(cols_pack.astype(jnp.bfloat16), (("gy", 1),), BRICK).astype(cols_pack.dtype)
    inner = ext_grad[:, BRICK:-BRICK]
    inner = inner.at[:, :BRICK].add(cols_back[:, :BRICK]).at[:, -BRICK:].add(cols_back[:, -BRICK:])
    rows_pack = jnp.concatenate([inner[:BRICK], inner[-BRICK:]], axis=0)
    rows_back = padded(rows_pack.astype(jnp.bfloat16), (("gx", 0),), BRICK).astype(rows_pack.dtype)
    core = inner[BRICK:-BRICK]
    core = core.at[:BRICK].add(rows_back[:BRICK]).at[-BRICK:].add(rows_back[-BRICK:])
    grad_kv = core.astype(jnp.bfloat16).reshape(tok_count, 2 * feat_width)
    grad_qkv = jnp.concatenate([grad_q_r.reshape(tok_count, feat_width), grad_kv], axis=1)
    grad_normed = lax.dot_general(
        grad_qkv, w_qkv, (((1,), (1,)), ((), ())), preferred_element_type=jnp.float32
    )
    all_tokens = tok_count * lax.axis_size("gx") * lax.axis_size("gy")
    inv_tokens = all_tokens ** (-0.5)
    w_grad_qkv = (
        lax.dot_general(
            normed, grad_qkv, (((0,), (0,)), ((), ())), preferred_element_type=jnp.float32
        )
        * inv_tokens
    )
    gain_grad = jnp.sum(grad_normed * flat_in * inv_rms, axis=0) * inv_tokens
    scaled = grad_normed * norm_gain
    grad_in = grad_flat.astype(jnp.float32) + inv_rms * (
        scaled - flat_in * inv_rms * inv_rms * jnp.mean(scaled * flat_in, axis=1, keepdims=True)
    )
    grad_in = grad_in.astype(jnp.bfloat16).reshape(fields.shape)
    shares = (
        lax.psum_scatter(w_grad_qkv, ("gx", "gy"), scatter_dimension=0, tiled=True),
        lax.psum_scatter(gain_grad, ("gx", "gy"), scatter_dimension=0, tiled=True),
    )
    return (output, grad_in, shares[0], shares[1])


def solution(mesh):
    placed = (P("gx", "gy", None), P("gx", "gy", None), P(), P(), P("gx", "gy", None))
    return jax.shard_map(
        per_device,
        mesh=mesh,
        in_specs=placed,
        out_specs=(
            P("gx", "gy", None),
            P("gx", "gy", None),
            P(("gx", "gy"), None),
            P(("gx", "gy")),
        ),
        check_vma=False,
    )
```

profile of v0, /device:TPU:1, one launch (start us, length us, event | category | flops | bytes accessed | tf_op | source)
XLA Modules:
  0.0 496.3 jit_solution(10697716485555818091)
XLA Ops:
  7.2 1.1 fusion.42
  8.4 1.1 fusion.38
  9.5 3.8 convolution_convert_fusion
  13.3 4.4 collective-permute-start.1
  17.7 18.4 %collective-permute-done.1 = bf16[8,16,2048]{2,1,0:T(8,128)(2,1)S(1)} collective-permute-done((bf16[8,16,2048]{2,1,0:T(8,128)(2,1)S(1)}, bf16[8,16,2048]{2,1,0:T(8,128)(2,1)S(1)}, u32[]{:S(2)}, u32[]{:S(2)}) %collective-permute-start.1) | collective-permute-done | bytes 524320 | tf_op jit(solution)/shard_map/ppermute | solution.py:22
  36.1 3.2 collective-permute-done
  39.5 1.3 fusion.60
  40.7 2.0 collective-permute-start.2
  43.1 0.7 slice.275
  44.0 0.3 reshape.320
  44.3 0.5 copy.135
  44.8 1.0 copy.176
  45.8 0.3 reshape.317
  46.2 1.3 copy.125
  47.4 4.6 collective-permute-done.2
  52.0 1.2 fusion.33
  53.3 1.7 collective-permute-done.3
  55.0 1.2 fusion.32
  56.7 0.7 copy.114
  57.4 1.9 fusion.57
  59.3 2.6 copy.117
  61.9 3.1 copy.115
  65.0 3.3 fusion.63
  68.3 6.2 %fusion.62 = (f32[2,16,64]{2,1,0:T(8,128)S(1)}, f32[2,16,64,576]{3,2,1,0:T(8,128)}) fusion(pred[2,576]{1,0:T(4,128)(4,1)S(1)} %gt.22, bf16[2,64,16,64]{1,3,2,0:T(8,128)(2,1)} %copy.125, bf16[2,576,16,64]{1,3,2,0:T(8,128)(2,1)} %bitcast.273), kind=kOutput, calls=%fused_computation.126 | convolution fusion | flops 155714112 | bytes 7349376 | tf_op jit(solution)/shard_map/sub | solution.py:94
  74.5 5.7 %convolution_bitcast_fusion = f32[1,2,576,16,64]{2,4,3,1,0:T(8,128)} fusion(bf16[2,64,16,64]{1,3,2,0:T(8,128)(2,1)S(1)} %copy.135, f32[2,16,64,576]{3,2,1,0:T(8,128)} %get-tuple-element.105, f32[2,16,64]{2,1,0:T(8,128)S(1)} %get-tuple-element.104), kind=kOutput, calls=%fused_computation.19 | convolution fusion | flops 153354240 | bytes 9707520 | tf_op jit(solution)/shard_map/abhqk,abqhd->abkhd/dot_general | solution.py:111
  80.2 20.0 %convolution_bitcast_fusion.1 = f32[1,2,576,16,64]{2,4,3,1,0:T(8,128)} fusion(bf16[2,64,16,64]{1,3,2,0:T(8,128)(2,1)S(1)} %copy-done.12, f32[2,16,576,64]{2,3,1,0:T(8,128)} %fusion.63, f32[2,16,64,576]{3,2,1,0:T(8,128)} %get-tuple-element.105, f32[2,16,64]{2,1,0:T(8,128)S(1)} %get-tuple-element.104), kind=kOutput, calls=%fused_computation.20 | convolution fusion | flops 159255104 | bytes 14426112 | tf_op jit(solution)/shard_map/abhqk,abqhd->abkhd/dot_general | solution.py:108
  100.2 8.5 %copy.136 = f32[1,2,576,16,64]{4,3,2,1,0:T(8,128)} copy(f32[1,2,576,16,64]{2,4,3,1,0:T(8,128)} %convolution_bitcast_fusion) | data formatting | bytes 9437184 | tf_op jit(solution)/shard_map/abhqk,abqhd->abkhd/transpose | solution.py:111
  108.7 8.8 %reshape.322 = f32[1,2,9,64,1024]{4,3,2,1,0:T(8,128)} reshape(f32[1,2,576,16,64]{4,3,2,1,0:T(8,128)} %copy.136) | data formatting | bytes 9437184 | tf_op jit(solution)/shard_map/reshape | solution.py:115
  117.6 3.8 slice_bitcast_fusion.8
  121.3 8.5 %copy.126 = f32[1,2,576,16,64]{4,3,2,1,0:T(8,128)} copy(f32[1,2,576,16,64]{2,4,3,1,0:T(8,128)} %convolution_bitcast_fusion.1) | data formatting | bytes 9437184 | tf_op jit(solution)/shard_map/abhqk,abqhd->abkhd/transpose | solution.py:108
  129.9 8.8 %reshape.321 = f32[1,2,9,64,1024]{4,3,2,1,0:T(8,128)} reshape(f32[1,2,576,16,64]{4,3,2,1,0:T(8,128)} %copy.126) | data formatting | bytes 9437184 | tf_op jit(solution)/shard_map/reshape | solution.py:114
  138.7 2.8 slice_bitcast_fusion.17
  141.5 1.1 pad_add_fusion
  142.6 0.8 maximum_bitcast_fusion
  143.4 0.4 copy.146
  143.8 0.5 convert.18
  144.4 0.8 collective-permute-start.4
  145.3 4.6 collective-permute-start.5
  149.9 0.2 slice.295
  150.1 4.1 collective-permute-done.4
  154.2 2.8 collective-permute-done.5
  157.2 0.4 fusion.11
  157.5 0.2 convert.19
  157.8 1.0 fusion.59
  158.8 2.2 collective-permute-start.6
  161.0 1.6 collective-permute-start.7
  162.6 20.5 %fusion.29 = bf16[1,2,64,16,64]{2,4,3,1,0:T(8,128)(2,1)} fusion(bf16[2,576,16,64]{1,3,2,0:T(8,128)(2,1)} %bitcast.274, f32[2,16,576,64]{2,3,1,0:T(8,128)} %fusion.63, f32[2,16,64,576]{3,2,1,0:T(8,128)} %get-tuple-element.105, f32[2,16,64]{2,1,0:T(8,128)S(1)} %get-tuple-element.104), kind=kOutput, calls=%fused_computation.36 | convolution fusion | flops 159386176 | bytes 12066816 | tf_op jit(solution)/shard_map/abhqk,abkhd->abqhd/dot_general | solution.py:105
  183.1 2.2 copy.123
  185.3 2.1 reshape_reshape.18
  187.5 1.0 copy.124
  188.5 1.5 fusion.31
  190.0 0.8 copy-done.6
  190.8 6.3 %convolution_multiply_fusion = f32[1024,3072]{1,0:T(8,128)} fusion(bf16[128,1024]{1,0:T(8,128)(2,1)S(1)} %fusion.38, bf16[128,2048]{1,0:T(8,128)(2,1)S(1)} %bitcast.275, bf16[128,1024]{1,0:T(8,128)(2,1)S(1)} %bitcast.280), kind=kOutput, calls=%fused_computation.2 | convolution fusion | flops 810024960 | bytes 13631488 | tf_op jit(solution)/shard_map/dot_general | solution.py:153
  197.1 1.7 copy-done.1
  198.8 4.5 fusion.26
  203.4 1.8 copy.119
  205.2 0.3 reshape.330
  205.5 0.8 fusion.35
  206.3 5.1 %fusion.45 = (f32[1024]{0:T(1024)S(1)}, f32[128]{0:T(128)S(1)}, f32[128,1024]{1,0:T(8,128)S(1)}) fusion(bf16[8,16,1024]{2,1,0:T(8,128)(2,1)S(1)} %copy-done.2, f32[128]{0:T(128)S(1)} %rsqrt.12, f32[1024]{0:T(1024)S(1)} %copy-done.13, bf16[1024,3072]{1,0:T(8,128)(2,1)} %param.20, bf16[128,2048]{1,0:T(8,128)(2,1)S(1)} %bitcast.276, ...), kind=kOutput, calls=%fused_computation.103 | convolution fusion | flops 807795584 | bytes 7873536 | tf_op jit(solution)/shard_map/dot_general | solution.py:147
  211.4 84.5 %all-reduce.19 = f32[1024]{0:T(1024)S(1)} all-reduce(f32[1024]{0:T(1024)S(1)} %broadcast_multiply_fusion), channel_id=3, replica_groups=mesh['gx'=8,'gy'=32] {'gx','gy'}, use_global_device_ids=true, to_apply=%region_7.8.clone | all-reduce | flops 1024 | bytes 8192
  295.9 0.6 dynamic-slice.27
  296.5 0.9 fusion.34
  297.4 190.5 %all-reduce.22.cloned.1.call-done = f32[1024,3072]{1,0:T(8,128)} async-done(((f32[1024,3072]{1,0:T(8,128)}), f32[1024,3072]{1,0:T(8,128)}) %all-reduce.22.cloned.1.call-update) | async-done | bytes 12582928
  487.9 1.5 constant_dynamic-slice_fusion
  (57 shorter events, 1.6 us)
Async XLA Ops:
  7.2 480.7 %all-reduce.22.cloned.1.call-start = ((), (), s32[]{:S(2)}) async-start(), calls=%async_computation | async-start | bytes 25165824
  13.3 29.6 %copy-start.14 = (s32[1,2,8]{2,1,0:T(2,128)S(1)}, s32[1,2,8]{2,1,0:T(2,128)}, u32[]{:S(2)}) copy-start(s32[1,2,8]{2,1,0:T(2,128)} %param.21) | copy-start | bytes 196
  13.3 29.6 %copy-start.8 = (bf16[8,16,1024]{2,1,0:T(8,128)(2,1)S(1)}, bf16[8,16,1024]{2,1,0:T(8,128)(2,1)}, u32[]{:S(2)}) copy-start(bf16[8,16,1024]{2,1,0:T(8,128)(2,1)} %param.18) | copy-start | bytes 786436
  13.3 22.8 %collective-permute-start.1 = (bf16[8,16,2048]{2,1,0:T(8,128)(2,1)S(1)}, bf16[8,16,2048]{2,1,0:T(8,128)(2,1)S(1)}, u32[]{:S(2)}, u32[]{:S(2)}) collective-permute-start(bf16[8,16,2048]{2,1,0:T(8,128)(2,1)S(1)} %bitcast.265), channel_id=1, source_target_pairs={{32,0},{64,32},{96,64},{128,96},{160,128},{192,160},{224,192},{0,2... | collective-permute-start | bytes 1572872 | tf_op jit(solution)/shard_map/ppermute | solution.py:22
  17.7 21.6 %collective-permute-start = (bf16[8,16,2048]{2,1,0:T(8,128)(2,1)S(1)}, bf16[8,16,2048]{2,1,0:T(8,128)(2,1)S(1)}, u32[]{:S(2)}, u32[]{:S(2)}) collective-permute-start(bf16[8,16,2048]{2,1,0:T(8,128)(2,1)S(1)} %bitcast.266), channel_id=1, source_target_pairs={{0,32},{32,64},{64,96},{96,128},{128,160},{160,192},{192,224},{224... | collective-permute-start | bytes 1572872 | tf_op jit(solution)/shard_map/ppermute | solution.py:21
  40.7 11.3 %collective-permute-start.2 = (bf16[24,8,2048]{2,1,0:T(8,128)(2,1)}, bf16[24,8,2048]{2,1,0:T(8,128)(2,1)}, u32[]{:S(2)}, u32[]{:S(2)}) collective-permute-start(bf16[24,8,2048]{2,1,0:T(8,128)(2,1)} %get-tuple-element.101), channel_id=1, source_target_pairs={{0,1},{1,2},{2,3},{3,4},{4,5},{5,6},{6,7},{7,8},{8,9},{9,10},{10,1... | collective-permute-start | bytes 2359304 | tf_op jit(solution)/shard_map/ppermute | solution.py:21
  42.9 12.1 %collective-permute-start.3 = (bf16[24,8,2048]{2,1,0:T(8,128)(2,1)}, bf16[24,8,2048]{2,1,0:T(8,128)(2,1)}, u32[]{:S(2)}, u32[]{:S(2)}) collective-permute-start(bf16[24,8,2048]{2,1,0:T(8,128)(2,1)} %get-tuple-element.100), channel_id=1, source_target_pairs={{1,0},{2,1},{3,2},{4,3},{5,4},{6,5},{7,6},{8,7},{9,8},{10,9},{11,1... | collective-permute-start | bytes 2359304 | tf_op jit(solution)/shard_map/ppermute | solution.py:22
  65.0 9.5 %copy-start = (bf16[1,2,576,1024]{2,3,1,0:T(8,128)(2,1)}, bf16[1,2,576,1024]{2,3,1,0:T(8,128)(2,1)S(1)}, u32[]{:S(2)}) copy-start(bf16[1,2,576,1024]{2,3,1,0:T(8,128)(2,1)S(1)} %copy.115) | copy-start | bytes 7077892
  74.5 5.7 %copy-start.12 = (bf16[2,64,16,64]{1,3,2,0:T(8,128)(2,1)S(1)}, bf16[2,64,16,64]{1,3,2,0:T(8,128)(2,1)}, u32[]{:S(2)}) copy-start(bf16[2,64,16,64]{1,3,2,0:T(8,128)(2,1)} %copy.125) | copy-start | bytes 786436
  138.7 2.8 copy-start.3
  138.7 2.8 copy-start.4
  138.7 2.8 copy-start.5
  144.4 9.8 %collective-permute-start.4 = (bf16[24,8,2048]{2,1,0:T(8,128)(2,1)S(1)}, bf16[24,8,2048]{2,1,0:T(8,128)(2,1)S(1)}, u32[]{:S(2)}, u32[]{:S(2)}) collective-permute-start(bf16[24,8,2048]{2,1,0:T(8,128)(2,1)S(1)} %get-tuple-element.90), channel_id=1, source_target_pairs={{0,1},{1,2},{2,3},{3,4},{4,5},{5,6},{6,7},{7,8},{8,9},{9,10},{10,1... | collective-permute-start | bytes 2359304 | tf_op jit(solution)/shard_map/ppermute | solution.py:21
  145.3 11.7 %collective-permute-start.5 = (bf16[24,8,2048]{2,1,0:T(8,128)(2,1)S(1)}, bf16[24,8,2048]{2,1,0:T(8,128)(2,1)S(1)}, u32[]{:S(2)}, u32[]{:S(2)}) collective-permute-start(bf16[24,8,2048]{2,1,0:T(8,128)(2,1)S(1)} %get-tuple-element.91), channel_id=1, source_target_pairs={{1,0},{2,1},{3,2},{4,3},{5,4},{6,5},{7,6},{8,7},{9,8},{10,9},{11,1... | collective-permute-start | bytes 2359304 | tf_op jit(solution)/shard_map/ppermute | solution.py:22
  158.8 29.7 %collective-permute-start.6 = (bf16[8,16,2048]{2,1,0:T(8,128)(2,1)}, bf16[8,16,2048]{2,1,0:T(8,128)(2,1)}, u32[]{:S(2)}, u32[]{:S(2)}) collective-permute-start(bf16[8,16,2048]{2,1,0:T(8,128)(2,1)} %get-tuple-element.98), channel_id=1, source_target_pairs={{0,32},{32,64},{64,96},{96,128},{128,160},{160,192},{192,224},{224... | collective-permute-start | bytes 1572872 | tf_op jit(solution)/shard_map/ppermute | solution.py:21
  161.0 27.5 %collective-permute-start.7 = (bf16[8,16,2048]{2,1,0:T(8,128)(2,1)}, bf16[8,16,2048]{2,1,0:T(8,128)(2,1)}, u32[]{:S(2)}, u32[]{:S(2)}) collective-permute-start(bf16[8,16,2048]{2,1,0:T(8,128)(2,1)} %get-tuple-element.99), channel_id=1, source_target_pairs={{32,0},{64,32},{96,64},{128,96},{160,128},{192,160},{224,192},{0,2... | collective-permute-start | bytes 1572872 | tf_op jit(solution)/shard_map/ppermute | solution.py:22
  188.4 1.6 copy-start.10
  190.0 0.8 copy-start.6
  197.1 1.7 copy-start.1
  198.8 6.7 %copy-start.2 = (bf16[8,16,1024]{2,1,0:T(8,128)(2,1)S(1)}, bf16[8,16,1024]{2,1,0:T(8,128)(2,1)}, u32[]{:S(2)}) copy-start(bf16[8,16,1024]{2,1,0:T(8,128)(2,1)} %param.17) | copy-start | bytes 786436
  203.4 2.9 copy-start.7
  203.4 2.9 copy-start.11
  203.4 2.9 copy-start.13
  205.5 91.0 %copy-start.9 = (bf16[8,16,1024]{2,1,0:T(8,128)(2,1)S(1)}, bf16[8,16,1024]{2,1,0:T(8,128)(2,1)}, u32[]{:S(2)}) copy-start(bf16[8,16,1024]{2,1,0:T(8,128)(2,1)} %param.18) | copy-start | bytes 786436
Sparse Core Ops, SparseCore 0:
  197.2 290.5 all-reduce.21
where the time goes:
time: 498 us; the launch traced here: 496 us
  waiting for transfers between devices  225 us (45%)
  blocking collectives  84.5 us (17%)
  matrix products  75.4 us (15%)
  local copies, waits for them, and re-layouts  69.7 us (14%)
  starting transfers between devices  15.8 us (3%)
  between operations  14.4 us (3%)
  other arithmetic  11.2 us (2%)
    unnamed x2, waiting for transfers between devices  190 us
    unnamed x1, blocking collectives  84.5 us
    ppermute x4, waiting for transfers between devices, padded(): after = lax.ppermute(first, axis, down)  22.9 us
    dot_general x1, matrix products, attend_both(): jnp.einsum('abhqk,abkhd->abqhd', grad_score, head_k, preferred_element_ty...  20.5 us
    dot_general x1, matrix products, attend_both(): jnp.einsum('abhqk,abqhd->abkhd', grad_score, head_q, preferred_element_ty...  20 us
    ppermute x4, waiting for transfers between devices, padded(): before = lax.ppermute(last, axis, up)  11.9 us
    ppermute x4, starting transfers between devices, padded(): after = lax.ppermute(first, axis, down)  10.7 us
  transfers between devices with their start and end apart: 9, of which 7 were waited for; matrix products, arithmetic and copies ran while one was open for 9% of the time, Pallas kernels for 0%

commit v1 on v0

v1 whole, which is shorter than its diff:
```python
import jax
import jax.numpy as jnp
from jax import lax
from jax.experimental import pallas as pl
from jax.experimental.pallas import tpu as pltpu
from jax.sharding import PartitionSpec as P

HEADS = 16
BRICK = 8
D = 1024
HD = 64
GROUP = 4
GW = GROUP * HD
INSIDE = BRICK * BRICK
OWN = 2 * INSIDE
EXT = 12 * INSIDE
EPSILON = 1e-05
NEG_BIG = -1e30
SCALE = HD ** (-0.5)
ALL_TOKENS = 32768
MESH = pl.DeviceIdType.MESH
F32 = jnp.float32
BF16 = jnp.bfloat16
ANY = pl.BlockSpec(memory_space=pl.ANY)
VM = pl.BlockSpec(memory_space=pltpu.VMEM)
VMEM_LIMIT = 56 * 1024 * 1024

COLUMN_OF = (1, 2, 3, 0)


def brick_of(tile, b):
    part = tile[:, BRICK * b : BRICK * (b + 1), :]
    return part.reshape(INSIDE, part.shape[-1])


def tile_of(bricks):
    width = bricks.shape[-1]
    first = bricks[:INSIDE].reshape(BRICK, BRICK, width)
    second = bricks[INSIDE:].reshape(BRICK, BRICK, width)
    return jnp.concatenate([first, second], axis=1)


def norm_kernel(fields_ref, grad_ref, gain_ref, nb_ref, nt_ref, gb_ref):
    x = fields_ref[...].astype(F32)
    x = jnp.concatenate([brick_of(x, 0), brick_of(x, 1)], axis=0)
    inv = lax.rsqrt(jnp.mean(x * x, axis=1, keepdims=True) + EPSILON)
    n = (x * inv * gain_ref[...]).astype(BF16)
    nb_ref[...] = n.reshape(2, INSIDE, D)
    nt_ref[...] = jnp.transpose(n.astype(F32)).astype(BF16)
    g = grad_ref[...].astype(F32)
    g = jnp.concatenate([brick_of(g, 0), brick_of(g, 1)], axis=0)
    gb_ref[...] = g.astype(BF16).reshape(2, INSIDE, D)


def norm_call(fields, grad_out, gain):
    return pl.pallas_call(
        norm_kernel,
        out_shape=(
            jax.ShapeDtypeStruct((2, INSIDE, D), BF16),
            jax.ShapeDtypeStruct((D, OWN), BF16),
            jax.ShapeDtypeStruct((2, INSIDE, D), BF16),
        ),
        in_specs=[VM] * 3,
        out_specs=(VM,) * 3,
        name="norm",
    )(fields, grad_out, gain)


def shifted(gx, gy, dx, dy):
    nx, ny = lax.axis_size("gx"), lax.axis_size("gy")
    return {"gx": lax.rem(gx + dx + nx, nx), "gy": lax.rem(gy + dy + ny, ny)}


def meet(peers):
    barrier = pltpu.get_barrier_semaphore()
    for peer in peers:
        pl.semaphore_signal(barrier, inc=1, device_id=peer, device_id_type=MESH)
    pl.semaphore_wait(barrier, len(peers))


def halo_kernel(nb, gb, nt, nrow, ncol, grow, gcol, ntp, send, recv):
    gx, gy = lax.axis_index("gx"), lax.axis_index("gy")
    up, down = shifted(gx, gy, -1, 0), shifted(gx, gy, 1, 0)
    left, right = shifted(gx, gy, 0, -1), shifted(gx, gy, 0, 1)
    partner = {"gx": gx, "gy": gy + 1 - 2 * lax.rem(gy, 2)}
    meet((up, down, left, right))

    def push(i, src, dst, peer):
        copy = pltpu.make_async_remote_copy(
            src_ref=src, dst_ref=dst, send_sem=send.at[i], recv_sem=recv.at[i],
            device_id=peer, device_id_type=MESH,
        )
        copy.start()
        return copy

    pending = []
    rows = []
    for a, (own, row, col) in enumerate(((nb, nrow, ncol), (gb, grow, gcol))):
        base = 8 * a
        to_up = push(base, own, row.at[1], up)
        to_down = push(base + 1, own, row.at[0], down)
        rows.append((to_down, to_up))
        pending.append(push(base + 2, own.at[0], col.at[0, 1], left))
        pending.append(push(base + 3, own.at[1], col.at[1, 1], right))
    pending.append(push(16, nt, ntp, partner))
    for a, (row, col) in enumerate(((nrow, ncol), (grow, gcol))):
        base = 8 * a + 4
        for side in range(2):
            rows[a][side].wait_recv()
            pending.append(push(base + 2 * side, row.at[side, 0], col.at[0, 2 * side], left))
            pending.append(push(base + 2 * side + 1, row.at[side, 1], col.at[1, 2 * side], right))
    for pair in rows:
        for copy in pair:
            copy.wait_send()
    for copy in pending:
        copy.wait()


def halo_call(nb, gb, nt):
    row = jax.ShapeDtypeStruct((2, 2, INSIDE, D), BF16)
    col = jax.ShapeDtypeStruct((2, 3, INSIDE, D), BF16)
    return pl.pallas_call(
        halo_kernel,
        out_shape=(row, col, row, col, jax.ShapeDtypeStruct((D, OWN), BF16)),
        in_specs=[ANY] * 3,
        out_specs=(ANY,) * 5,
        scratch_shapes=[pltpu.SemaphoreType.DMA((17,)), pltpu.SemaphoreType.DMA((17,))],
        compiler_params=pltpu.CompilerParams(collective_id=0, has_side_effects=True),
        name="halo",
    )(nb, gb, nt)


def assemble(dst, own, row, col):
    for r in range(3):
        base = 4 * INSIDE * r
        middle = own[...] if r == 1 else row[r // 2]
        dst[base : base + OWN, :] = middle.reshape(OWN, middle.shape[-1])
        dst[base + OWN : base + OWN + INSIDE, :] = col[0, r]
        dst[base + OWN + INSIDE : base + 2 * OWN, :] = col[1, r]


def head_lanes(shape):
    return lax.broadcasted_iota(jnp.int32, shape, 1) // HD


def spread_heads(block):
    lanes = head_lanes(block.shape)
    zero = jnp.zeros_like(block)
    return jnp.concatenate([jnp.where(lanes == h, block, zero) for h in range(GROUP)], axis=0)


def pick_heads(stacked):
    lanes = head_lanes((OWN, GW))
    out = stacked[:OWN]
    for h in range(1, GROUP):
        out = jnp.where(lanes == h, stacked[OWN * h : OWN * (h + 1)], out)
    return out


def dot(a, b):
    return lax.dot_general(a, b, (((1,), (0,)), ((), ())), preferred_element_type=F32)


def dot_t(a, b):
    return lax.dot_general(a, b, (((1,), (1,)), ((), ())), preferred_element_type=F32)


def attend_kernel(
    mask_ref, nb, nrow, ncol, wq, wk, wv, gb, fields_ref,
    out_ref, dq_ref, q_ref, k_ref, v_ref, stats_ref,
    n_ext, s_buf, dp_buf, w_buf, ds_buf,
):
    g = pl.program_id(0)

    @pl.when(g == 0)
    def _():
        assemble(n_ext, nb, nrow, ncol)
        lane = lax.broadcasted_iota(jnp.int32, (1, OWN), 1)
        for j in range(8):
            row = jnp.where(lane < INSIDE, mask_ref[0, j], mask_ref[1, j])
            stats_ref[32 + j : 33 + j, :] = row.astype(F32)

    n = n_ext[...]
    q4 = dot(n, wq[...]).astype(BF16)
    k4 = dot(n, wk[...]).astype(BF16)
    v4 = dot(n, wv[...]).astype(BF16)
    q_ref[...] = q4
    mine = slice(4 * INSIDE, 4 * INSIDE + OWN)
    k_ref[...] = k4[mine]
    v_ref[...] = v4[mine]
    grad = gb[...].reshape(OWN, GW)
    s_buf[...] = dot_t(spread_heads(q4[mine]), k4)
    dp_buf[...] = dot_t(spread_heads(grad), v4)

    place = lax.broadcasted_iota(jnp.int32, (1, EXT), 1) // INSIDE
    masks = []
    for b in range(2):
        allowed = jnp.zeros((1, EXT), jnp.int32)
        for r in range(3):
            for p in range(4):
                c = COLUMN_OF[p] - b
                if c < 0 or c > 2:
                    continue
                m = 3 * r + c
                value = 1 if m == 4 else mask_ref[b, m if m < 4 else m - 1]
                allowed = jnp.where(place == 4 * r + p, value, allowed)
        masks.append(jnp.broadcast_to(allowed, (INSIDE, EXT)))
    allowed = jnp.concatenate(masks, axis=0) > 0

    lane = lax.broadcasted_iota(jnp.int32, (OWN, OWN), 1)
    stat = jnp.zeros((OWN, OWN), F32)
    for h in range(GROUP):
        part = slice(OWN * h, OWN * (h + 1))
        s = jnp.where(allowed, s_buf[part, :] * SCALE, NEG_BIG)
        top = jnp.max(s, axis=1, keepdims=True)
        e = jnp.exp(s - top)
        total = jnp.sum(e, axis=1, keepdims=True)
        p = e * (1.0 / total)
        w_buf[part, :] = p.astype(BF16)
        dp = dp_buf[part, :]
        inner = jnp.sum(p * dp, axis=1, keepdims=True)
        ds_buf[part, :] = (p * (dp - inner) * SCALE).astype(BF16)
        stat = jnp.where(lane == h, top + jnp.log(total), stat)
        stat = jnp.where(lane == GROUP + h, inner, stat)
    stats_ref[pl.ds(pl.multiple_of(8 * g, 8), 8), :] = jnp.transpose(stat)[0:8]

    mixed = pick_heads(dot(w_buf[...], v4)).astype(BF16).astype(F32)
    dq_ref[...] = pick_heads(dot(ds_buf[...], k4)).astype(BF16)
    out_ref[...] = (fields_ref[...].astype(F32) + tile_of(mixed)).astype(BF16)


def attend_call(mask, nb, nrow, ncol, w, gb, fields):
    fixed3 = pl.BlockSpec((2, INSIDE, D), lambda g: (0, 0, 0), pipeline_mode=pl.Buffered(1))
    return pl.pallas_call(
        attend_kernel,
        grid=(HEADS // GROUP,),
        out_shape=(
            jax.ShapeDtypeStruct(fields.shape, BF16),
            jax.ShapeDtypeStruct((OWN, D), BF16),
            jax.ShapeDtypeStruct((EXT, D), BF16),
            jax.ShapeDtypeStruct((OWN, D), BF16),
            jax.ShapeDtypeStruct((OWN, D), BF16),
            jax.ShapeDtypeStruct((40, OWN), F32),
        ),
        in_specs=[
            pl.BlockSpec(memory_space=pltpu.SMEM),
            fixed3,
            pl.BlockSpec((2, 2, INSIDE, D), lambda g: (0, 0, 0, 0), pipeline_mode=pl.Buffered(1)),
            pl.BlockSpec((2, 3, INSIDE, D), lambda g: (0, 0, 0, 0), pipeline_mode=pl.Buffered(1)),
            pl.BlockSpec((D, GW), lambda g: (0, g)),
            pl.BlockSpec((D, GW), lambda g: (0, g + 4)),
            pl.BlockSpec((D, GW), lambda g: (0, g + 8)),
            pl.BlockSpec((2, INSIDE, GW), lambda g: (0, 0, g)),
            pl.BlockSpec((BRICK, 2 * BRICK, GW), lambda g: (0, 0, g)),
        ],
        out_specs=(
            pl.BlockSpec((BRICK, 2 * BRICK, GW), lambda g: (0, 0, g)),
            pl.BlockSpec((OWN, GW), lambda g: (0, g)),
            pl.BlockSpec((EXT, GW), lambda g: (0, g)),
            pl.BlockSpec((OWN, GW), lambda g: (0, g)),
            pl.BlockSpec((OWN, GW), lambda g: (0, g)),
            pl.BlockSpec((40, OWN), lambda g: (0, 0)),
        ),
        scratch_shapes=[
            pltpu.VMEM((EXT, D), BF16),
            pltpu.VMEM((GROUP * OWN, EXT), F32),
            pltpu.VMEM((GROUP * OWN, EXT), F32),
            pltpu.VMEM((GROUP * OWN, EXT), BF16),
            pltpu.VMEM((GROUP * OWN, EXT), BF16),
        ],
        compiler_params=pltpu.CompilerParams(vmem_limit_bytes=VMEM_LIMIT),
        name="attend",
    )(mask, nb, nrow, ncol, w, w, w, gb, fields)


def stats_kernel(own, ext, send, recv):
    gx, gy = lax.axis_index("gx"), lax.axis_index("gy")
    spots = [i for i in range(9) if i != 4]
    peers = [shifted(gx, gy, i // 3 - 1, i % 3 - 1) for i in spots]
    meet(peers)
    copies = []
    for i, peer in zip(spots, peers):
        copy = pltpu.make_async_remote_copy(
            src_ref=own, dst_ref=ext.at[8 - i], send_sem=send.at[i], recv_sem=recv.at[i],
            device_id=peer, device_id_type=MESH,
        )
        copy.start()
        copies.append(copy)
    for copy in copies:
        copy.wait()


def stats_call(stats):
    return pl.pallas_call(
        stats_kernel,
        out_shape=jax.ShapeDtypeStruct((9, 40, OWN), F32),
        in_specs=[ANY],
        out_specs=ANY,
        scratch_shapes=[pltpu.SemaphoreType.DMA((9,)), pltpu.SemaphoreType.DMA((9,))],
        compiler_params=pltpu.CompilerParams(collective_id=1, has_side_effects=True),
        name="stats",
    )(stats)


def keys_kernel(
    stats, st_ext, q_ref, k_ref, v_ref, gb, grow, gcol, dq_ref, wq, wk, wv,
    fields_ref, grad_ref, gain_ref,
    dk_ref, dv_ref, gin_ref, ggain_ref,
    g_ext, s_buf, dp_buf, w_buf, ds_buf, gn_buf,
):
    g = pl.program_id(0)
    assemble(g_ext, gb, grow, gcol)
    q4 = q_ref[...]
    g4 = g_ext[...]
    s_buf[...] = dot_t(spread_heads(k_ref[...]), q4)
    dp_buf[...] = dot_t(spread_heads(v_ref[...]), g4)

    def lanes_of(first):
        low = lax.broadcasted_iota(jnp.int32, (8, OWN), 1) < INSIDE
        parts = []
        for r in range(3):
            rows = pl.ds(first, 8)
            middle = stats[rows, :] if r == 1 else st_ext[3 * r + 1, rows, :]
            parts += [middle, jnp.where(low, st_ext[3 * r + 2, rows, :], st_ext[3 * r, rows, :])]
        return jnp.concatenate(parts, axis=1)

    stat = lanes_of(pl.multiple_of(8 * g, 8))
    brick_masks = lanes_of(32)
    place = lax.broadcasted_iota(jnp.int32, (1, EXT), 1) // INSIDE
    masks = []
    for b in range(2):
        allowed = jnp.zeros((1, EXT), F32)
        for r in range(3):
            for p in range(4):
                c = b + 2 - COLUMN_OF[p]
                if c < 0 or c > 2:
                    continue
                m = 3 * (2 - r) + c
                if m == 4:
                    value = jnp.ones((1, EXT), F32)
                else:
                    j = m if m < 4 else m - 1
                    value = brick_masks[j : j + 1, :]
                allowed = jnp.where(place == 4 * r + p, value, allowed)
        masks.append(jnp.broadcast_to(allowed, (INSIDE, EXT)))
    allowed = jnp.concatenate(masks, axis=0) > 0.5

    for h in range(GROUP):
        part = slice(OWN * h, OWN * (h + 1))
        s = jnp.where(allowed, s_buf[part, :] * SCALE - stat[h : h + 1, :], NEG_BIG)
        p = jnp.exp(s)
        w_buf[part, :] = p.astype(BF16)
        inner = stat[GROUP + h : GROUP + h + 1, :]
        ds_buf[part, :] = (p * (dp_buf[part, :] - inner) * SCALE).astype(BF16)

    dv = pick_heads(dot(w_buf[...], g4)).astype(BF16)
    dk = pick_heads(dot(ds_buf[...], q4)).astype(BF16)
    dk_ref[...] = dk
    dv_ref[...] = dv
    step = dot_t(dq_ref[...], wq[...]) + dot_t(dk, wk[...]) + dot_t(dv, wv[...])

    @pl.when(g == 0)
    def _():
        gn_buf[...] = step

    @pl.when(g > 0)
    def _():
        gn_buf[...] += step

    @pl.when(g == HEADS // GROUP - 1)
    def _():
        gn = gn_buf[...]
        x = fields_ref[...].astype(F32)
        x = jnp.concatenate([brick_of(x, 0), brick_of(x, 1)], axis=0)
        inv = lax.rsqrt(jnp.mean(x * x, axis=1, keepdims=True) + EPSILON)
        total = jnp.sum(gn * x * inv, axis=0, keepdims=True)
        for i in range(8):
            ggain_ref[i : i + 1, :] = total[:, 128 * i : 128 * (i + 1)]
        s = gn * gain_ref[...]
        back = inv * (s - x * inv * inv * jnp.mean(s * x, axis=1, keepdims=True))
        gin_ref[...] = (grad_ref[...].astype(F32) + tile_of(back)).astype(BF16)


def keys_call(stats, st_ext, q, k, v, gb, grow, gcol, dq, w, fields, grad_out, gain):
    own = pl.BlockSpec((OWN, GW), lambda g: (0, g))
    tile = pl.BlockSpec((BRICK, 2 * BRICK, D), lambda g: (0, 0, 0), pipeline_mode=pl.Buffered(1))
    return pl.pallas_call(
        keys_kernel,
        grid=(HEADS // GROUP,),
        out_shape=(
            jax.ShapeDtypeStruct((OWN, D), BF16),
            jax.ShapeDtypeStruct((OWN, D), BF16),
            jax.ShapeDtypeStruct(fields.shape, BF16),
            jax.ShapeDtypeStruct((8, 128), F32),
        ),
        in_specs=[
            pl.BlockSpec((40, OWN), lambda g: (0, 0)),
            pl.BlockSpec((9, 40, OWN), lambda g: (0, 0, 0)),
            pl.BlockSpec((EXT, GW), lambda g: (0, g)),
            own,
            own,
            pl.BlockSpec((2, INSIDE, GW), lambda g: (0, 0, g)),
            pl.BlockSpec((2, 2, INSIDE, GW), lambda g: (0, 0, 0, g)),
            pl.BlockSpec((2, 3, INSIDE, GW), lambda g: (0, 0, 0, g)),
            own,
            pl.BlockSpec((D, GW), lambda g: (0, g)),
            pl.BlockSpec((D, GW), lambda g: (0, g + 4)),
            pl.BlockSpec((D, GW), lambda g: (0, g + 8)),
            tile,
            tile,
            pl.BlockSpec((1, D), lambda g: (0, 0)),
        ],
        out_specs=(
            own,
            own,
            pl.BlockSpec((BRICK, 2 * BRICK, D), lambda g: (0, 0, 0)),
            pl.BlockSpec((8, 128), lambda g: (0, 0)),
        ),
        scratch_shapes=[
            pltpu.VMEM((EXT, GW), BF16),
            pltpu.VMEM((GROUP * OWN, EXT), F32),
            pltpu.VMEM((GROUP * OWN, EXT), F32),
            pltpu.VMEM((GROUP * OWN, EXT), BF16),
            pltpu.VMEM((GROUP * OWN, EXT), BF16),
            pltpu.VMEM((OWN, D), F32),
        ],
        compiler_params=pltpu.CompilerParams(vmem_limit_bytes=VMEM_LIMIT),
        name="keys",
    )(stats, st_ext, q, k, v, gb, grow, gcol, dq, w, w, w, fields, grad_out, gain)


CW = 768


def reduce_kernel(
    dq, dk, dv, nt, ntp, gain,
    out, gout,
    b_recv, w_send, r1, s1, r2, s2, r3, fin, r4,
    h1, t1, h2, t2, h3, t3, h4,
    bs, br, s1s, s1r, s2s, s2r, s3s, s3r, s4s, s4r,
):
    gx, gy = lax.axis_index("gx"), lax.axis_index("gy")
    x = gx // 2
    yi = 2 * lax.rem(gx, 2) + gy // 16
    z = lax.rem(gy, 16) // 2
    core = lax.rem(gy, 2)

    def device(x_, yi_, z_, core_):
        return {"gx": 2 * x_ + yi_ // 2, "gy": 16 * lax.rem(yi_, 2) + 2 * z_ + core_}

    partner = device(x, yi, z, 1 - core)
    x_at = [lax.rem(x + d, 4) for d in range(4)]
    y_at = [lax.rem(yi + d, 4) for d in range(4)]
    z_at = [lax.rem(z + d, 8) for d in range(8)]
    x_peer = [device(x_at[d], yi, z, core) for d in range(4)]
    y_peer = [device(x, y_at[d], z, core) for d in range(4)]
    z_peer = [device(x, yi, z_at[d], core) for d in range(8)]
    meet([partner] + x_peer[1:] + y_peer[1:] + z_peer[1:])

    def push(src, dst, send, recv, peer):
        copy = pltpu.make_async_remote_copy(
            src_ref=src, dst_ref=dst, send_sem=send, recv_sem=recv,
            device_id=peer, device_id_type=MESH,
        )
        copy.start()
        return copy

    sources = (dq, dk, dv)
    first = []
    for colour in range(2):
        for t in range(3):
            cols = pl.ds(pl.multiple_of(512 * (1 - core) + 256 * colour, 256), 256)
            at = CW * colour + 256 * t
            i = 3 * colour + t
            first.append(
                push(sources[t].at[:, cols], b_recv.at[:, at : at + 256], bs.at[i], br.at[i], partner)
            )
    for copy in first:
        copy.wait()

    own_b = []
    for colour in range(2):
        cols = pl.ds(pl.multiple_of(512 * core + 256 * colour, 256), 256)
        own_b.append(jnp.concatenate([ref[:, cols] for ref in sources], axis=1))

    def block(colour, row):
        rows = pl.ds(pl.multiple_of(64 * row, 64), 64)
        return dot(nt[rows, :], own_b[colour]) + dot(
            ntp[rows, :], b_recv[:, CW * colour : CW * (colour + 1)]
        )

    stage1 = []
    for slot, d in enumerate((2, 1, 3)):
        for i in range(4):
            w_send[0, slot, i] = block(0, 4 * x_at[d] + i).astype(BF16)
            w_send[1, slot, i] = block(1, 4 * i + y_at[d]).astype(BF16)
        stage1.append(push(w_send.at[0, slot], r1.at[0, slot], s1s.at[slot], s1r.at[slot], x_peer[d]))
        stage1.append(
            push(w_send.at[1, slot], r1.at[1, slot], s1s.at[3 + slot], s1r.at[3 + slot], y_peer[d])
        )
        stage1.append(push(gain, h1.at[slot], s1s.at[6 + slot], s1r.at[6 + slot], x_peer[d]))
    for copy in stage1:
        copy.wait()

    for i in range(4):
        acc = block(0, 4 * x + i)
        for slot in range(3):
            acc = acc + r1[0, slot, i].astype(F32)
        s1[0, i] = acc.astype(BF16)
        acc = block(1, 4 * i + yi)
        for slot in range(3):
            acc = acc + r1[1, slot, i].astype(F32)
        s1[1, i] = acc.astype(BF16)
    t1[...] = gain[...] + h1[0] + h1[1] + h1[2]

    stage2 = []
    for slot, d in enumerate((2, 1, 3)):
        stage2.append(push(s1.at[0, y_at[d]], r2.at[0, slot], s2s.at[slot], s2r.at[slot], y_peer[d]))
        stage2.append(
            push(s1.at[1, x_at[d]], r2.at[1, slot], s2s.at[3 + slot], s2r.at[3 + slot], x_peer[d])
        )
        stage2.append(push(t1, h2.at[slot], s2s.at[6 + slot], s2r.at[6 + slot], y_peer[d]))
    for copy in stage2:
        copy.wait()

    for colour, mine in ((0, yi), (1, x)):
        acc = s1[colour, mine].astype(F32)
        for slot in range(3):
            acc = acc + r2[colour, slot].astype(F32)
        for zz in range(8):
            s2[zz, :, CW * colour : CW * (colour + 1)] = acc[8 * zz : 8 * zz + 8].astype(BF16)
    t2[...] = t1[...] + h2[0] + h2[1] + h2[2]

    stage3 = []
    for slot, d in enumerate((4, 3, 5, 2, 6, 1, 7)):
        stage3.append(push(s2.at[z_at[d]], r3.at[slot], s3s.at[slot], s3r.at[slot], z_peer[d]))
        stage3.append(push(t2, h3.at[slot], s3s.at[7 + slot], s3r.at[7 + slot], z_peer[d]))
    for copy in stage3:
        copy.wait()

    acc = s2[z].astype(F32)
    tot = t2[...]
    for slot in range(7):
        acc = acc + r3[slot].astype(F32)
        tot = tot + h3[slot]
    t3[...] = tot
    acc = acc * (ALL_TOKENS ** (-0.5))
    fin[0] = acc[0:4]
    fin[1] = acc[4:8]
    last = [
        push(fin.at[1 - core], r4, s4s.at[0], s4r.at[0], partner),
        push(t3, h4, s4s.at[1], s4r.at[1], partner),
    ]
    for copy in last:
        copy.wait()
    gout[...] = (t3[...] + h4[...]) * (ALL_TOKENS ** (-0.5))
    mine, other = fin[core], r4[...]
    is_first = jnp.broadcast_to(core, mine.shape) == 0
    halves = (jnp.where(is_first, mine, other), jnp.where(is_first, other, mine))
    for t in range(3):
        for half in range(2):
            for colour in range(2):
                to = 1024 * t + 512 * half + 256 * colour
                at = CW * colour + 256 * t
                out[:, to : to + 256] = halves[half][:, at : at + 256]


def reduce_call(dq, dk, dv, nt, ntp, gain):
    dma = pltpu.SemaphoreType.DMA
    tile = (8, 128)
    return pl.pallas_call(
        reduce_kernel,
        out_shape=(jax.ShapeDtypeStruct((4, 3 * D), F32), jax.ShapeDtypeStruct(tile, F32)),
        in_specs=[VM] * 6,
        out_specs=(VM, VM),
        scratch_shapes=[
            pltpu.VMEM((OWN, 2 * CW), BF16),
            pltpu.VMEM((2, 3, 4, 64, CW), BF16),
            pltpu.VMEM((2, 3, 4, 64, CW), BF16),
            pltpu.VMEM((2, 4, 64, CW), BF16),
            pltpu.VMEM((2, 3, 64, CW), BF16),
            pltpu.VMEM((8, 8, 2 * CW), BF16),
            pltpu.VMEM((7, 8, 2 * CW), BF16),
            pltpu.VMEM((2, 4, 2 * CW), F32),
            pltpu.VMEM((4, 2 * CW), F32),
            pltpu.VMEM((3,) + tile, F32),
            pltpu.VMEM(tile, F32),
            pltpu.VMEM((3,) + tile, F32),
            pltpu.VMEM(tile, F32),
            pltpu.VMEM((7,) + tile, F32),
            pltpu.VMEM(tile, F32),
            pltpu.VMEM(tile, F32),
            dma((6,)), dma((6,)),
            dma((9,)), dma((9,)),
            dma((9,)), dma((9,)),
            dma((14,)), dma((14,)),
            dma((2,)), dma((2,)),
        ],
        compiler_params=pltpu.CompilerParams(
            collective_id=2, has_side_effects=True, vmem_limit_bytes=VMEM_LIMIT
        ),
        name="reduce",
    )(dq, dk, dv, nt, ntp, gain)


def per_device(fields, grad_out, norm_gain, w_qkv, brick_mask):
    gain = norm_gain.reshape(1, D)
    mask = brick_mask.reshape(2, 8)
    nb, nt, gb = norm_call(fields, grad_out, gain)
    nrow, ncol, grow, gcol, ntp = halo_call(nb, gb, nt)
    output, dq, q, k, v, stats = attend_call(mask, nb, nrow, ncol, w_qkv, gb, fields)
    st_ext = stats_call(stats)
    dk, dv, grad_in, ggain = keys_call(
        stats, st_ext, q, k, v, gb, grow, gcol, dq, w_qkv, fields, grad_out, gain
    )
    w_grad, gain_sum = reduce_call(dq, dk, dv, nt, ntp, ggain)
    owner = lax.axis_index("gx") * lax.axis_size("gy") + lax.axis_index("gy")
    gain_grad = lax.dynamic_slice(gain_sum.reshape(D), (4 * owner,), (4,))
    return (output, grad_in, w_grad, gain_grad)


def solution(mesh):
    placed = (P("gx", "gy", None), P("gx", "gy", None), P(), P(), P("gx", "gy", None))
    return jax.shard_map(
        per_device,
        mesh=mesh,
        in_specs=placed,
        out_specs=(
            P("gx", "gy", None),
            P("gx", "gy", None),
            P(("gx", "gy"), None),
            P(("gx", "gy")),
        ),
        check_vma=False,
    )
```

time: 498 us -> 131 us (0.26)
  waiting for transfers between devices: 225 us -> 0 us
  Pallas kernels: 0 us -> 128 us
  blocking collectives: 84.5 us -> 0 us
  matrix products: 75.4 us -> 0 us
  local copies, waits for them, and re-layouts: 69.7 us -> 2.69 us
  starting transfers between devices: 15.8 us -> 0 us
  between operations: 14.4 us -> 0.67 us
  other arithmetic: 11.2 us -> 0 us
    unnamed x2 -> x0, waiting for transfers between devices: 190 us -> none
    pallas_call x0 -> x6, Pallas kernels: none -> 128 us  [the longest x1 47.4 us: reduce_call(): pl.pallas_call(reduce_kernel, out_shape=(jax.ShapeDtypeStruct((4, 3 * D),...]
    unnamed x1 -> x0, blocking collectives: 84.5 us -> none
    dot_general x8 -> x0, matrix products: 69.2 us -> none  [the longest x1 20.5 us: attend_both(): jnp.einsum('abhqk,abkhd->abqhd', grad_score, head_k, preferred_element_ty...]
    ppermute x8 -> x0, waiting for transfers between devices: 34.8 us -> none  [the longest x4 22.9 us: padded(): after = lax.ppermute(first, axis, down)]
    transpose x5 -> x0, local copies, waits for them, and re-layouts: 18.5 us -> none  [the longest x1 8.52 us: attend_both(): jnp.einsum('abhqk,abqhd->abkhd', weights, grad_head, preferred_element_ty...]
    reshape x2 -> x0, local copies, waits for them, and re-layouts: 17.7 us -> none  [the longest x1 8.83 us: attend_both(): grad_k = grad_k.reshape(b_rows, b_cols, 9, inside, feat_width)]
    ppermute x8 -> x0, starting transfers between devices: 15.7 us -> none  [the longest x4 10.7 us: padded(): after = lax.ppermute(first, axis, down)]
  transfers between devices with their start and end apart: 9 -> 0, of which waited for: 7 -> 0; matrix products, arithmetic and copies ran while one was open for 9% -> 0% of each run, Pallas kernels for 0% -> 0%
where the time goes in v1:
time: 131 us
  Pallas kernels  128 us (98%)
  local copies, waits for them, and re-layouts  2.69 us (2%)
    pallas_call x1, Pallas kernels, reduce_call(): pl.pallas_call(reduce_kernel, out_shape=(jax.ShapeDtypeStruct((4, 3 * D),...  47.4 us
    pallas_call x1, Pallas kernels, halo_call(): pl.pallas_call(halo_kernel, out_shape=(row, col, row, col, jax.ShapeDtype...  34.5 us
    pallas_call x1, Pallas kernels, stats_call(): pl.pallas_call(stats_kernel, out_shape=jax.ShapeDtypeStruct((9, 40, OWN),...  18.1 us
    pallas_call x1, Pallas kernels, attend_call(): pl.pallas_call(attend_kernel, grid=(HEADS // GROUP,), out_shape=(jax.Shap...  14.9 us
    pallas_call x1, Pallas kernels, keys_call(): pl.pallas_call(keys_kernel, grid=(HEADS // GROUP,), out_shape=(jax.ShapeD...  10.5 us

profile of v1, /device:TPU:1, one launch (start us, length us, event | category | flops | bytes accessed | tf_op | source)
XLA Modules:
  0.0 130.9 jit_solution(4691301634278706241)
XLA Ops:
  0.6 2.1 %norm.1 = (bf16[2,64,1024]{2,1,0:T(8,128)(2,1)}, bf16[1024,128]{1,0:T(8,128)(2,1)}, bf16[2,64,1024]{2,1,0:T(8,128)(2,1)}) custom-call(bf16[8,16,1024]{2,1,0:T(8,128)(2,1)} %fields_ref.5, bf16[8,16,1024]{2,1,0:T(8,128)(2,1)} %grad_ref.3, f32[1,1024]{1,0:T(1,128)} %bitcast.3), custom_call_target="tpu_custom_call" | custom-call | tf_op jit(solution)/shard_map/norm/pallas_call | solution.py:56
  2.7 34.5 %halo.1 = (bf16[2,2,64,1024]{3,2,1,0:T(8,128)(2,1)}, bf16[2,3,64,1024]{3,2,1,0:T(8,128)(2,1)}, bf16[2,2,64,1024]{3,2,1,0:T(8,128)(2,1)}, bf16[2,3,64,1024]{3,2,1,0:T(8,128)(2,1)}, bf16[1024,128]{1,0:T(8,128)(2,1)}) custom-call(bf16[2,64,1024]{2,1,0:T(8,128)(2,1)} %get-tuple-element.24.nb, bf16[2,64,1024]{2,1,0:T(8,128)(2,1)} %get-tuple-element.25.gb, ...), custom_call_target="tpu_custom_call" | custom-call | tf_op jit(solution)/shard_map/halo/pallas_call | solution.py:122
  37.3 14.9 %attend.1 = (bf16[8,16,1024]{2,1,0:T(8,128)(2,1)}, bf16[128,1024]{1,0:T(8,128)(2,1)}, bf16[768,1024]{1,0:T(8,128)(2,1)}, bf16[128,1024]{1,0:T(8,128)(2,1)}, bf16...) custom-call(s32[2,8]{1,0:T(2,128)} %bitcast.5, bf16[2,64,1024]{2,1,0:T(8,128)(2,1)} %get-tuple-element.24.nb, ...), custom_call_target="tpu_custom_call" | custom-call | tf_op jit(solution)/shard_map/attend/pallas_call | solution.py:234
  52.1 18.1 %stats.1.st_ext = f32[9,40,128]{2,1,0:T(8,128)} custom-call(f32[40,128]{1,0:T(8,128)} %get-tuple-element.30.own.stats), custom_call_target="tpu_custom_call" | custom-call | tf_op jit(solution)/shard_map/stats/pallas_call | solution.py:294
  70.2 10.5 %keys.1 = (bf16[128,1024]{1,0:T(8,128)(2,1)}, bf16[128,1024]{1,0:T(8,128)(2,1)}, bf16[8,16,1024]{2,1,0:T(8,128)(2,1)}, f32[8,128]{1,0:T(8,128)}) custom-call(f32[40,128]{1,0:T(8,128)} %get-tuple-element.30.own.stats, f32[9,40,128]{2,1,0:T(8,128)} %stats.1.st_ext, bf16[768,1024]{1,0:T(8,128)(2,1)} %get-tuple-element.31.q_ref, ...), custom_call_target="tpu_custom_call" | custom-call | tf_op jit(solution)/shard_map/keys/pallas_call | solution.py:387
  80.8 47.4 %reduce.1 = (f32[4,3072]{1,0:T(4,128)}, f32[8,128]{1,0:T(8,128)}) custom-call(bf16[128,1024]{1,0:T(8,128)(2,1)} %get-tuple-element.36.dq_ref.dq, bf16[128,1024]{1,0:T(8,128)(2,1)} %get-tuple-element.38.dk, bf16[128,1024]{1,0:T(8,128)(2,1)} %get-tuple-element.39.dv, bf16[1024,128]{1,0:T(8,128)(2,1)} %get-tuple-element.26.nt, ...), custom_call_target="tpu_custom_call" | custom-call | tf_op jit(solution)/shard_map/reduce/pallas_call | solution.py:571
  128.2 1.3 dynamic_slice.3
  129.4 1.4 %copy.10 = f32[4,3072]{1,0:T(4,128)} copy(f32[4,3072]{1,0:T(4,128)} %get-tuple-element.50) | data formatting | bytes 98304

commit v2 on v0

v2 whole, which is shorter than its diff:
```python
import jax
import jax.numpy as jnp
from jax import lax
from jax.experimental import pallas as pl
from jax.experimental.pallas import tpu as pltpu
from jax.sharding import PartitionSpec as P

HEADS = 16
BRICK = 8
D = 1024
HD = 64
GROUP = 4
GW = GROUP * HD
INSIDE = BRICK * BRICK
OWN = 2 * INSIDE
EXT = 12 * INSIDE
EPSILON = 1e-05
NEG_BIG = -1e30
SCALE = HD ** (-0.5)
ALL_TOKENS = 32768
MESH = pl.DeviceIdType.MESH
F32 = jnp.float32
BF16 = jnp.bfloat16
ANY = pl.BlockSpec(memory_space=pl.ANY)
VM = pl.BlockSpec(memory_space=pltpu.VMEM)
SM = pl.BlockSpec(memory_space=pltpu.SMEM)
VMEM_LIMIT = 56 * 1024 * 1024

COLUMN_OF = (1, 2, 3, 0)


def brick_of(tile, b):
    part = tile[:, BRICK * b : BRICK * (b + 1), :]
    return part.reshape(INSIDE, part.shape[-1])


def tile_of(bricks):
    width = bricks.shape[-1]
    first = bricks[:INSIDE].reshape(BRICK, BRICK, width)
    second = bricks[INSIDE:].reshape(BRICK, BRICK, width)
    return jnp.concatenate([first, second], axis=1)


def shifted(gx, gy, dx, dy):
    nx, ny = lax.axis_size("gx"), lax.axis_size("gy")
    return {"gx": lax.rem(gx + dx + nx, nx), "gy": lax.rem(gy + dy + ny, ny)}


def dot(a, b):
    return lax.dot_general(a, b, (((1,), (0,)), ((), ())), preferred_element_type=F32)


def dot_t(a, b):
    return lax.dot_general(a, b, (((1,), (1,)), ((), ())), preferred_element_type=F32)


def head_lanes(shape):
    return lax.broadcasted_iota(jnp.int32, shape, 1) // HD


def spread_heads(block):
    lanes = head_lanes(block.shape)
    zero = jnp.zeros_like(block)
    return jnp.concatenate([jnp.where(lanes == h, block, zero) for h in range(GROUP)], axis=0)


def pick_heads(stacked):
    lanes = head_lanes((OWN, GW))
    out = stacked[:OWN]
    for h in range(1, GROUP):
        out = jnp.where(lanes == h, stacked[OWN * h : OWN * (h + 1)], out)
    return out


def bricks_of(tile):
    return jnp.concatenate([brick_of(tile, 0), brick_of(tile, 1)], axis=0)


def at(index, size):
    start = index * size
    return pl.ds(start if isinstance(start, int) else pl.multiple_of(start, size), size)


def steps(first, last, body):
    if UNROLL:
        for g in range(first, last):
            body(g)
    else:

        def once(g, carry):
            body(g)
            return carry

        lax.fori_loop(first, last, once, 0)


UNROLL = False
GROUPS = HEADS // GROUP
HW = GW // 2
CW = 3 * HW
SPOTS = (0, 1, 2, 3, 5, 6, 7, 8)
PLACE = 4 * INSIDE
MINE = slice(PLACE, PLACE + OWN)
HALO, STAT, PAIR, ONE, TWO, THREE, FOUR, SEMS = 0, 17, 62, 66, 93, 120, 134, 136


def layer_kernel(
    mask_ref, fields_ref, grad_ref, gain_ref, w_hbm,
    out_ref, gin_ref, wg_ref, gg_ref,
    w, n_ext, g_ext, a2, q_ext, k_ext, v_ext, dq_all, dk_all, dv_all,
    s_buf, dp_buf, w_buf, ds_buf, stats, st_ext,
    b_own, b_other, w_send, r1, s1, r2, s2, r3, fin, r4,
    h0, h1, t1, h2, t2, h3, t3, h4,
    load_sem, send, recv,
):
    gx, gy = lax.axis_index("gx"), lax.axis_index("gy")
    up, down = shifted(gx, gy, -1, 0), shifted(gx, gy, 1, 0)
    left, right = shifted(gx, gy, 0, -1), shifted(gx, gy, 0, 1)
    around = [shifted(gx, gy, i // 3 - 1, i % 3 - 1) for i in SPOTS]
    x, yi = gx // 2, 2 * lax.rem(gx, 2) + gy // 16
    z, core = lax.rem(gy, 16) // 2, lax.rem(gy, 2)

    def device(x_, yi_, z_, core_):
        return {"gx": 2 * x_ + yi_ // 2, "gy": 16 * lax.rem(yi_, 2) + 2 * z_ + core_}

    partner = device(x, yi, z, 1 - core)
    x_at = [lax.rem(x + d, 4) for d in range(4)]
    y_at = [lax.rem(yi + d, 4) for d in range(4)]
    z_at = [lax.rem(z + d, 8) for d in range(8)]
    x_peer = [device(x_at[d], yi, z, core) for d in range(4)]
    y_peer = [device(x, y_at[d], z, core) for d in range(4)]
    z_peer = [device(x, yi, z_at[d], core) for d in range(8)]

    def copy_of(i, src, dst, peer):
        return pltpu.make_async_remote_copy(
            src_ref=src, dst_ref=dst, send_sem=send.at[i], recv_sem=recv.at[i],
            device_id=peer, device_id_type=MESH,
        )

    sent = []

    def push(i, src, dst, peer):
        copy = copy_of(i, src, dst, peer)
        copy.start()
        sent.append(copy)
        return copy

    loads = [
        pltpu.make_async_copy(w_hbm.at[:, at(t, D)], w.at[:, at(t, D)], load_sem.at[t])
        for t in range(3)
    ]
    for load in loads:
        load.start()

    peers = around + x_peer[1:] + y_peer[1:] + z_peer[1:]
    barrier = pltpu.get_barrier_semaphore()
    for peer in peers:
        pl.semaphore_signal(barrier, inc=1, device_id=peer, device_id_type=MESH)

    xf = bricks_of(fields_ref[...].astype(F32))
    inv = lax.rsqrt(jnp.mean(xf * xf, axis=1, keepdims=True) + EPSILON)
    n = (xf * inv * gain_ref[...]).astype(BF16)
    n_ext[1, 0:2] = n.reshape(2, INSIDE, D)
    a2[0] = jnp.transpose(n.astype(F32)).astype(BF16)
    g_ext[1, 0:2] = bricks_of(grad_ref[...].astype(F32)).astype(BF16).reshape(2, INSIDE, D)
    lane = lax.broadcasted_iota(jnp.int32, (1, OWN), 1)
    for j in range(8):
        row = jnp.where(lane < INSIDE, mask_ref[0, j], mask_ref[1, j])
        stats[32 + j : 33 + j, :] = row.astype(F32)
    pl.semaphore_wait(barrier, len(peers))

    def send_rows(base, ext):
        to_up = push(base, ext.at[1, 0:2], ext.at[2, 0:2], up)
        to_down = push(base + 1, ext.at[1, 0:2], ext.at[0, 0:2], down)
        return [
            (to_down, to_up),
            push(base + 2, ext.at[1, 0], ext.at[1, 2], left),
            push(base + 3, ext.at[1, 1], ext.at[1, 3], right),
        ]

    def send_corners(base, ext, pair):
        out = []
        for side in range(2):
            r = 2 * side
            pair[side].wait_recv()
            out.append(push(base + 4 + r, ext.at[r, 0], ext.at[r, 2], left))
            out.append(push(base + 5 + r, ext.at[r, 1], ext.at[r, 3], right))
        return out

    def stat_copy(i, g, peer):
        rows = at(g, 8)
        return copy_of(STAT + 9 * g + i, stats.at[rows, :], st_ext.at[8 - i, rows, :], peer)

    n_pair, *n_cols = send_rows(HALO, n_ext)
    a2_copy = push(16, a2.at[0], a2.at[1], partner)
    for i, peer in zip(SPOTS, around):
        stat_copy(i, GROUPS, peer).start()

    def project(rows, targets):
        def one(j):
            for t, dst in enumerate((q_ext, k_ext, v_ext)):
                part = pl.ds(pl.multiple_of(D * t + GW * j, GW), GW)
                made = dot(rows, w[:, part]).astype(BF16)
                for i, to in enumerate(targets):
                    dst[to : to + OWN, at(j, GW)] = made[OWN * i : OWN * (i + 1)]

        def once(j, carry):
            one(j)
            return carry

        lax.fori_loop(0, GROUPS, once, 0)

    for load in loads:
        load.wait()
    project(n_ext[1, 0:2].reshape(OWN, D), (PLACE,))
    n_cols += send_corners(HALO, n_ext, n_pair)
    g_pair, *g_cols = send_rows(HALO + 8, g_ext)
    project(
        jnp.concatenate([n_ext[r, 0:2].reshape(OWN, D) for r in (0, 2)], axis=0), (0, 2 * PLACE)
    )
    for copy in n_cols:
        copy.wait_recv()
    project(
        jnp.concatenate([n_ext[r, 2:4].reshape(OWN, D) for r in range(3)], axis=0),
        (OWN, PLACE + OWN, 2 * PLACE + OWN),
    )

    place = lax.broadcasted_iota(jnp.int32, (1, EXT), 1) // INSIDE

    def attend(g):
        cols = at(g, GW)
        k4, v4 = k_ext[:, cols], v_ext[:, cols]
        s_buf[...] = dot_t(spread_heads(q_ext[MINE, cols]), k4)
        dp_buf[...] = dot_t(spread_heads(g_ext[1, 0:2, :, cols].reshape(OWN, GW)), v4)
        masks = []
        for b in range(2):
            allowed = jnp.zeros((1, EXT), jnp.int32)
            for r in range(3):
                for p in range(4):
                    c = COLUMN_OF[p] - b
                    if c < 0 or c > 2:
                        continue
                    m = 3 * r + c
                    value = 1 if m == 4 else mask_ref[b, m if m < 4 else m - 1]
                    allowed = jnp.where(place == 4 * r + p, value, allowed)
            masks.append(jnp.broadcast_to(allowed, (INSIDE, EXT)))
        allowed = jnp.concatenate(masks, axis=0) > 0
        lane = lax.broadcasted_iota(jnp.int32, (OWN, OWN), 1)
        stat = jnp.zeros((OWN, OWN), F32)
        for h in range(GROUP):
            part = slice(OWN * h, OWN * (h + 1))
            s = jnp.where(allowed, s_buf[part, :] * SCALE, NEG_BIG)
            top = jnp.max(s, axis=1, keepdims=True)
            e = jnp.exp(s - top)
            total = jnp.sum(e, axis=1, keepdims=True)
            p = e * (1.0 / total)
            w_buf[part, :] = p.astype(BF16)
            dp = dp_buf[part, :]
            inner = jnp.sum(p * dp, axis=1, keepdims=True)
            ds_buf[part, :] = (p * (dp - inner) * SCALE).astype(BF16)
            stat = jnp.where(lane == h, top + jnp.log(total), stat)
            stat = jnp.where(lane == GROUP + h, inner, stat)
        stats[at(g, 8), :] = jnp.transpose(stat)[0:8]
        for i, peer in zip(SPOTS, around):
            stat_copy(i, g, peer).start()
        mixed = pick_heads(dot(w_buf[...], v4)).astype(BF16).astype(F32)
        dq_all[:, cols] = pick_heads(dot(ds_buf[...], k4)).astype(BF16)
        out_ref[:, :, cols] = (fields_ref[:, :, cols].astype(F32) + tile_of(mixed)).astype(BF16)

    steps(0, 2, attend)
    g_cols += send_corners(HALO + 8, g_ext, g_pair)
    steps(2, GROUPS, attend)

    for copy in g_cols + [a2_copy]:
        copy.wait_recv()
    for i, peer in zip(SPOTS, around):
        stat_copy(i, GROUPS, peer).wait()

    def lanes_of(g):
        low = lax.broadcasted_iota(jnp.int32, (8, OWN), 1) < INSIDE
        rows = at(g, 8)
        parts = []
        for r in range(3):
            middle = stats[rows, :] if r == 1 else st_ext[3 * r + 1, rows, :]
            parts += [middle, jnp.where(low, st_ext[3 * r + 2, rows, :], st_ext[3 * r, rows, :])]
        return jnp.concatenate(parts, axis=1)

    def pair_copy(g):
        return copy_of(PAIR + g, b_own.at[g, 1 - core], b_other.at[g], partner)

    def one_copies(g):
        out = []
        for slot, d in enumerate((2, 1, 3)):
            base = ONE + 6 * g + slot
            out.append(copy_of(base, w_send.at[g, x_at[d], :, 0], r1.at[g, 0, slot], x_peer[d]))
            out.append(copy_of(base + 3, w_send.at[g, :, y_at[d], 1], r1.at[g, 1, slot], y_peer[d]))
        return out

    def weigh(g):
        pair_copy(g).wait()
        both = jnp.concatenate([b_own[g, core], b_other[g]], axis=0)
        for part in range(4):
            rows = slice(256 * part, 256 * (part + 1))
            left_side = jnp.concatenate([a2[0, rows, :], a2[1, rows, :]], axis=1)
            w_send[g, part] = dot(left_side, both).astype(BF16).reshape(4, 2, 32, CW)
        for copy in one_copies(g):
            copy.start()

    def keys(g):
        cols = at(g, GW)
        for i, peer in zip(SPOTS, around):
            stat_copy(i, g, peer).wait()
        q4 = q_ext[:, cols]
        g4 = g_ext[:, :, :, cols].reshape(EXT, GW)
        s_buf[...] = dot_t(spread_heads(k_ext[MINE, cols]), q4)
        dp_buf[...] = dot_t(spread_heads(v_ext[MINE, cols]), g4)
        stat, brick_masks = lanes_of(g), lanes_of(GROUPS)
        masks = []
        for b in range(2):
            allowed = jnp.zeros((1, EXT), F32)
            for r in range(3):
                for p in range(4):
                    c = b + 2 - COLUMN_OF[p]
                    if c < 0 or c > 2:
                        continue
                    m = 3 * (2 - r) + c
                    j = m if m < 4 else m - 1
                    value = jnp.ones((1, EXT), F32) if m == 4 else brick_masks[j : j + 1, :]
                    allowed = jnp.where(place == 4 * r + p, value, allowed)
            masks.append(jnp.broadcast_to(allowed, (INSIDE, EXT)))
        allowed = jnp.concatenate(masks, axis=0) > 0.5
        for h in range(GROUP):
            part = slice(OWN * h, OWN * (h + 1))
            s = jnp.where(allowed, s_buf[part, :] * SCALE - stat[h : h + 1, :], NEG_BIG)
            p = jnp.exp(s)
            w_buf[part, :] = p.astype(BF16)
            inner = stat[GROUP + h : GROUP + h + 1, :]
            ds_buf[part, :] = (p * (dp_buf[part, :] - inner) * SCALE).astype(BF16)
        dv4 = pick_heads(dot(w_buf[...], g4)).astype(BF16)
        dk4 = pick_heads(dot(ds_buf[...], q4)).astype(BF16)
        dk_all[:, cols] = dk4
        dv_all[:, cols] = dv4
        dq4 = dq_all[:, cols]
        for half in range(2):
            b_own[g, half] = jnp.concatenate(
                [value[:, HW * half : HW * (half + 1)] for value in (dq4, dk4, dv4)], axis=1
            )
        pair_copy(g).start()
        if isinstance(g, int):
            if g > 0:
                weigh(g - 1)
        else:
            pl.when(g > 0)(lambda: weigh(g - 1))

    steps(0, GROUPS, keys)
    weigh(GROUPS - 1)

    grads = (dq_all[...], dk_all[...], dv_all[...])
    parts = []
    for j in range(4):
        rows = at(j, GW)
        made = dot_t(grads[0], w[rows, 0:D])
        made = made + dot_t(grads[1], w[rows, D : 2 * D])
        parts.append(made + dot_t(grads[2], w[rows, 2 * D : 3 * D]))
    gn = jnp.concatenate(parts, axis=1)
    xf = bricks_of(fields_ref[...].astype(F32))
    inv = lax.rsqrt(jnp.mean(xf * xf, axis=1, keepdims=True) + EPSILON)
    total = jnp.sum(gn * xf * inv, axis=0, keepdims=True)
    for i in range(8):
        h0[i : i + 1, :] = total[:, 128 * i : 128 * (i + 1)]
    for slot, d in enumerate((2, 1, 3)):
        push(ONE + 24 + slot, h0, h1.at[slot], x_peer[d])
    s = gn * gain_ref[...]
    back = inv * (s - xf * inv * inv * jnp.mean(s * xf, axis=1, keepdims=True))
    gin_ref[...] = (grad_ref[...].astype(F32) + tile_of(back)).astype(BF16)

    two = []
    for g in range(GROUPS):
        for copy in one_copies(g):
            copy.wait()
        for i in range(4):
            acc = w_send[g, x, i, 0].astype(F32)
            for slot in range(3):
                acc = acc + r1[g, 0, slot, i].astype(F32)
            s1[g, 0, i] = acc.astype(BF16)
            acc = w_send[g, i, yi, 1].astype(F32)
            for slot in range(3):
                acc = acc + r1[g, 1, slot, i].astype(F32)
            s1[g, 1, i] = acc.astype(BF16)
        mine = []
        for slot, d in enumerate((2, 1, 3)):
            base = TWO + 6 * g + slot
            mine.append(push(base, s1.at[g, 0, y_at[d]], r2.at[g, 0, slot], y_peer[d]))
            mine.append(push(base + 3, s1.at[g, 1, x_at[d]], r2.at[g, 1, slot], x_peer[d]))
        two.append(mine)

    gains = [copy_of(ONE + 24 + slot, h0, h1.at[slot], x_peer[1]) for slot in range(3)]
    for copy in gains:
        copy.wait_recv()
    t1[...] = h0[...] + h1[0] + h1[1] + h1[2]
    gains = []
    for slot, d in enumerate((2, 1, 3)):
        gains.append(push(TWO + 24 + slot, t1, h2.at[slot], y_peer[d]))

    for g in range(GROUPS):
        for copy in two[g]:
            copy.wait_recv()
        for colour, mine in ((0, yi), (1, x)):
            acc = s1[g, colour, mine].astype(F32)
            for slot in range(3):
                acc = acc + r2[g, colour, slot].astype(F32)
            for zz in range(4):
                s2[4 * colour + zz, :, CW * g : CW * (g + 1)] = acc[8 * zz : 8 * zz + 8].astype(BF16)
    for copy in gains:
        copy.wait_recv()
    t2[...] = t1[...] + h2[0] + h2[1] + h2[2]

    three = []
    for slot, d in enumerate((4, 3, 5, 2, 6, 1, 7)):
        three.append(push(THREE + slot, s2.at[z_at[d]], r3.at[slot], z_peer[d]))
        three.append(push(THREE + 7 + slot, t2, h3.at[slot], z_peer[d]))
    for copy in three:
        copy.wait_recv()
    acc = s2[z].astype(F32)
    tot = t2[...]
    for slot in range(7):
        acc = acc + r3[slot].astype(F32)
        tot = tot + h3[slot]
    t3[...] = tot
    acc = acc * (ALL_TOKENS ** (-0.5))
    fin[0] = acc[0:4]
    fin[1] = acc[4:8]
    four = [push(FOUR, fin.at[1 - core], r4, partner), push(FOUR + 1, t3, h4, partner)]
    for copy in four:
        copy.wait_recv()
    gg_ref[...] = (t3[...] + h4[...]) * (ALL_TOKENS ** (-0.5))
    mine, other = fin[core], r4[...]
    is_first = jnp.broadcast_to(core, mine.shape) == 0
    halves = (jnp.where(is_first, mine, other), jnp.where(is_first, other, mine))
    for g in range(GROUPS):
        for t in range(3):
            for half in range(2):
                to = D * t + GW * g + HW * half
                come = CW * g + HW * t
                wg_ref[:, to : to + HW] = halves[half][:, come : come + HW]
    for copy in sent:
        copy.wait_send()


def layer_call(mask, fields, grad_out, gain, w):
    dma = pltpu.SemaphoreType.DMA
    vm = pltpu.VMEM
    tile = (8, 128)
    stack = (GROUP * OWN, EXT)
    return pl.pallas_call(
        layer_kernel,
        out_shape=(
            jax.ShapeDtypeStruct(fields.shape, BF16),
            jax.ShapeDtypeStruct(fields.shape, BF16),
            jax.ShapeDtypeStruct((4, 3 * D), F32),
            jax.ShapeDtypeStruct(tile, F32),
        ),
        in_specs=[SM, VM, VM, VM, ANY],
        out_specs=(VM,) * 4,
        scratch_shapes=[
            vm((D, 3 * D), BF16),
            vm((3, 4, INSIDE, D), BF16), vm((3, 4, INSIDE, D), BF16),
            vm((2, D, OWN), BF16),
            vm((EXT, D), BF16), vm((EXT, D), BF16), vm((EXT, D), BF16),
            vm((OWN, D), BF16), vm((OWN, D), BF16), vm((OWN, D), BF16),
            vm(stack, F32), vm(stack, F32), vm(stack, BF16), vm(stack, BF16),
            vm((40, OWN), F32), vm((9, 40, OWN), F32),
            vm((GROUPS, 2, OWN, CW), BF16), vm((GROUPS, OWN, CW), BF16),
            vm((GROUPS, 4, 4, 2, 32, CW), BF16),
            vm((GROUPS, 2, 3, 4, 32, CW), BF16),
            vm((GROUPS, 2, 4, 32, CW), BF16),
            vm((GROUPS, 2, 3, 32, CW), BF16),
            vm((8, 8, GROUPS * CW), BF16),
            vm((7, 8, GROUPS * CW), BF16),
            vm((2, 4, GROUPS * CW), F32),
            vm((4, GROUPS * CW), F32),
            vm(tile, F32), vm((3,) + tile, F32),
            vm(tile, F32), vm((3,) + tile, F32),
            vm(tile, F32), vm((7,) + tile, F32),
            vm(tile, F32), vm(tile, F32),
            dma((3,)), dma((SEMS,)), dma((SEMS,)),
        ],
        compiler_params=pltpu.CompilerParams(
            collective_id=0, has_side_effects=True, vmem_limit_bytes=VMEM_LIMIT
        ),
        name="layer",
    )(mask, fields, grad_out, gain, w)


def per_device(fields, grad_out, norm_gain, w_qkv, brick_mask):
    output, grad_in, w_grad, gain_sum = layer_call(
        brick_mask.reshape(2, 8), fields, grad_out, norm_gain.reshape(1, D), w_qkv
    )
    owner = lax.axis_index("gx") * lax.axis_size("gy") + lax.axis_index("gy")
    gain_grad = lax.dynamic_slice(gain_sum.reshape(D), (4 * owner,), (4,))
    return (output, grad_in, w_grad, gain_grad)


def solution(mesh):
    placed = (P("gx", "gy", None), P("gx", "gy", None), P(), P(), P("gx", "gy", None))
    return jax.shard_map(
        per_device,
        mesh=mesh,
        in_specs=placed,
        out_specs=(
            P("gx", "gy", None),
            P("gx", "gy", None),
            P(("gx", "gy"), None),
            P(("gx", "gy")),
        ),
        check_vma=False,
    )
```

time: 498 us -> 98.5 us (0.20)
  waiting for transfers between devices: 225 us -> 0 us
  Pallas kernels: 0 us -> 91.6 us
  blocking collectives: 84.5 us -> 0 us
  matrix products: 75.4 us -> 0 us
  local copies, waits for them, and re-layouts: 69.7 us -> 6.03 us
  starting transfers between devices: 15.8 us -> 0 us
  between operations: 14.4 us -> 0.65 us
  other arithmetic: 11.2 us -> 0 us
    unnamed x2 -> x0, waiting for transfers between devices: 190 us -> none
    pallas_call x0 -> x1, Pallas kernels: none -> 91.6 us  [layer_call(): pl.pallas_call(layer_kernel, out_shape=(jax.ShapeDtypeStruct(fields.shape...]
    unnamed x1 -> x0, blocking collectives: 84.5 us -> none
    dot_general x8 -> x0, matrix products: 69.2 us -> none  [the longest x1 20.5 us: attend_both(): jnp.einsum('abhqk,abkhd->abqhd', grad_score, head_k, preferred_element_ty...]
    ppermute x8 -> x0, waiting for transfers between devices: 34.8 us -> none  [the longest x4 22.9 us: padded(): after = lax.ppermute(first, axis, down)]
    transpose x5 -> x0, local copies, waits for them, and re-layouts: 18.5 us -> none  [the longest x1 8.52 us: attend_both(): jnp.einsum('abhqk,abqhd->abkhd', weights, grad_head, preferred_element_ty...]
    reshape x2 -> x0, local copies, waits for them, and re-layouts: 17.7 us -> none  [the longest x1 8.83 us: attend_both(): grad_k = grad_k.reshape(b_rows, b_cols, 9, inside, feat_width)]
    ppermute x8 -> x0, starting transfers between devices: 15.7 us -> none  [the longest x4 10.7 us: padded(): after = lax.ppermute(first, axis, down)]
  transfers between devices with their start and end apart: 9 -> 0, of which waited for: 7 -> 0; matrix products, arithmetic and copies ran while one was open for 9% -> 0% of each run, Pallas kernels for 0% -> 0%
where the time goes in v2:
time: 98.5 us; the launch traced here: 98.3 us
  Pallas kernels  91.6 us (93%)
  local copies, waits for them, and re-layouts  6.03 us (6%)
    pallas_call x1, Pallas kernels, layer_call(): pl.pallas_call(layer_kernel, out_shape=(jax.ShapeDtypeStruct(fields.shape...  91.6 us
    unnamed x3, local copies, waits for them, and re-layouts  4.76 us

profile of v2, /device:TPU:1, one launch (start us, length us, event | category | flops | bytes accessed | tf_op | source)
XLA Modules:
  0.0 98.3 jit_solution(15032384324326370499)
XLA Ops:
  0.6 91.6 %layer.1 = (bf16[8,16,1024]{2,1,0:T(8,128)(2,1)}, bf16[8,16,1024]{2,1,0:T(8,128)(2,1)}, f32[4,3072]{1,0:T(4,128)}, f32[8,128]{1,0:T(8,128)}) custom-call(s32[2,8]{1,0:T(2,128)} %bitcast.4, bf16[8,16,1024]{2,1,0:T(8,128)(2,1)} %fields_ref.1, bf16[8,16,1024]{2,1,0:T(8,128)(2,1)} %grad_ref.1, f32[1,1024]{1,0:T(1,128)} %bitcast.3, bf16[1024,3072]{1,0:T(8,128)(2,1)} %w_hbm.1), custom_call_target="tpu_custom_call" | custom-call | tf_op jit(solution)/shard_map/layer/pallas_call | solution.py:455
  92.2 1.3 %dynamic_slice.3 = f32[4]{0:T(128)} dynamic-slice(f32[1024]{0:T(1024)} %bitcast.5, s32[]{:T(128)S(6)} %select_n.3), dynamic_slice_sizes={4} | dynamic-slice | bytes 36 | tf_op jit(solution)/shard_map/dynamic_slice | solution.py:500
  93.5 1.7 %copy.12 = bf16[8,16,1024]{2,1,0:T(8,128)(2,1)} copy(bf16[8,16,1024]{2,1,0:T(8,128)(2,1)} %get-tuple-element.16) | data formatting | bytes 524288
  95.2 1.7 %copy.13 = bf16[8,16,1024]{2,1,0:T(8,128)(2,1)} copy(bf16[8,16,1024]{2,1,0:T(8,128)(2,1)} %get-tuple-element.17) | data formatting | bytes 524288
  96.9 1.4 %copy.14 = f32[4,3072]{1,0:T(4,128)} copy(f32[4,3072]{1,0:T(4,128)} %get-tuple-element.18) | data formatting | bytes 98304

commit v3 on v2

v3 whole, which is shorter than its diff:
```python
import jax
import jax.numpy as jnp
from jax import lax
from jax.experimental import pallas as pl
from jax.experimental.pallas import tpu as pltpu
from jax.sharding import PartitionSpec as P

HEADS = 16
BRICK = 8
D = 1024
HD = 64
GROUP = 4
GW = GROUP * HD
INSIDE = BRICK * BRICK
OWN = 2 * INSIDE
EXT = 12 * INSIDE
EPSILON = 1e-05
NEG_BIG = -1e30
SCALE = HD ** (-0.5)
ALL_TOKENS = 32768
MESH = pl.DeviceIdType.MESH
F32 = jnp.float32
BF16 = jnp.bfloat16
ANY = pl.BlockSpec(memory_space=pl.ANY)
VM = pl.BlockSpec(memory_space=pltpu.VMEM)
SM = pl.BlockSpec(memory_space=pltpu.SMEM)
VMEM_LIMIT = 56 * 1024 * 1024

ROW_OF = (1, 0, 2)
COLUMN_OF = (1, 2, 3, 0)


def brick_of(tile, b):
    part = tile[:, BRICK * b : BRICK * (b + 1), :]
    return part.reshape(INSIDE, part.shape[-1])


def tile_of(bricks):
    width = bricks.shape[-1]
    first = bricks[:INSIDE].reshape(BRICK, BRICK, width)
    second = bricks[INSIDE:].reshape(BRICK, BRICK, width)
    return jnp.concatenate([first, second], axis=1)


def shifted(gx, gy, dx, dy):
    nx, ny = lax.axis_size("gx"), lax.axis_size("gy")
    return {"gx": lax.rem(gx + dx + nx, nx), "gy": lax.rem(gy + dy + ny, ny)}


def dot(a, b):
    return lax.dot_general(a, b, (((1,), (0,)), ((), ())), preferred_element_type=F32)


def dot_t(a, b):
    return lax.dot_general(a, b, (((1,), (1,)), ((), ())), preferred_element_type=F32)


def head_lanes(shape):
    return lax.broadcasted_iota(jnp.int32, shape, 1) // HD


def spread_heads(block):
    lanes = head_lanes(block.shape)
    zero = jnp.zeros_like(block)
    return jnp.concatenate([jnp.where(lanes == h, block, zero) for h in range(GROUP)], axis=0)


def pick_heads(stacked):
    lanes = head_lanes((OWN, GW))
    out = stacked[:OWN]
    for h in range(1, GROUP):
        out = jnp.where(lanes == h, stacked[OWN * h : OWN * (h + 1)], out)
    return out


def bricks_of(tile):
    return jnp.concatenate([brick_of(tile, 0), brick_of(tile, 1)], axis=0)


def at(index, size):
    start = index * size
    return pl.ds(start if isinstance(start, int) else pl.multiple_of(start, size), size)


def steps(first, last, body):
    def once(g, carry):
        body(g)
        return carry

    lax.fori_loop(first, last, once, 0)


GROUPS = HEADS // GROUP
HW = GW // 2
UNITS = 6
UW = 2 * HW
SPOTS = (0, 1, 2, 3, 5, 6, 7, 8)
MINE = slice(0, OWN)
SIBLINGS = (2, 1, 3)
FAR_FIRST = (4, 3, 5, 2, 6, 1, 7)
(N_NEAR, N_FAR, N_MID, N_CORNER, G_NEAR, G_FAR, G_MID, G_CORNER, A2, STAT, PAIR, ONE, TWO, THREE,
 FOUR, GAIN, SEMS) = (0, 4, 6, 7, 8, 10, 12, 13, 14, 15, 20, 26, 32, 38, 40, 41, 45)


def layer_kernel(
    mask_ref, fields_ref, grad_ref, gain_ref, w_hbm,
    out_hbm, gin_hbm, wg_ref, gg_ref,
    w, n_ext, g_ext, a2, q_ext, k_ext, v_ext, dq_all, dk_all, dv_all,
    s_buf, dp_buf, w_buf, ds_buf, stats, st_ext, out_v, gin_v,
    b_own, b_other, w_send, r1, s1, r2, s2, r3, fin, r4,
    h0, h1, t1, h2, t2, h3, t3, h4,
    local_sem, send, recv,
):
    gx, gy = lax.axis_index("gx"), lax.axis_index("gy")
    left, right = shifted(gx, gy, 0, -1), shifted(gx, gy, 0, 1)
    around = [shifted(gx, gy, i // 3 - 1, i % 3 - 1) for i in SPOTS]
    odd = lax.rem(gx, 2)
    x, yi = gx // 2, 2 * odd + gy // 16
    z, core = lax.rem(gy, 16) // 2, lax.rem(gy, 2)

    def device(x_, yi_, z_, core_):
        return {"gx": 2 * x_ + yi_ // 2, "gy": 16 * lax.rem(yi_, 2) + 2 * z_ + core_}

    partner = device(x, yi, z, 1 - core)
    x_at = [lax.rem(x + d, 4) for d in range(4)]
    y_at = [lax.rem(yi + d, 4) for d in range(4)]
    z_at = [lax.rem(z + d, 8) for d in range(8)]
    x_peer = [device(x_at[d], yi, z, core) for d in range(4)]
    y_peer = [device(x, y_at[d], z, core) for d in range(4)]
    z_peer = [device(x, yi, z_at[d], core) for d in range(8)]
    mate = {"gx": gx + 1 - 2 * odd, "gy": gy}
    onward = {"gx": lax.rem(gx + 2 + 4 * odd, 8), "gy": gy}
    near, far = 2 - odd, 1 + odd

    def copy_of(i, src, dst, peer):
        return pltpu.make_async_remote_copy(
            src_ref=src, dst_ref=dst, send_sem=send.at[i], recv_sem=recv.at[i],
            device_id=peer, device_id_type=MESH,
        )

    def push(i, src, dst, peer):
        copy_of(i, src, dst, peer).start()

    def arrive(i, ref):
        copy_of(i, ref, ref, partner).wait_recv()

    def leave(i, ref):
        copy_of(i, ref, ref, partner).wait_send()

    loads = [
        pltpu.make_async_copy(w_hbm.at[:, at(t, D)], w.at[:, at(t, D)], local_sem.at[t])
        for t in range(3)
    ]
    for load in loads:
        load.start()

    peers = around + x_peer[1:] + y_peer[1:] + z_peer[1:]
    barrier = pltpu.get_barrier_semaphore()
    for peer in peers:
        pl.semaphore_signal(barrier, inc=1, device_id=peer, device_id_type=MESH)

    xf = bricks_of(fields_ref[...].astype(F32))
    inv = lax.rsqrt(jnp.mean(xf * xf, axis=1, keepdims=True) + EPSILON)
    n = (xf * inv * gain_ref[...]).astype(BF16)
    n_ext[0, 0:2] = n.reshape(2, INSIDE, D)
    a2[0] = jnp.transpose(n.astype(F32)).astype(BF16)
    g_ext[0, 0:2] = bricks_of(grad_ref[...].astype(F32)).astype(BF16).reshape(2, INSIDE, D)
    lane = lax.broadcasted_iota(jnp.int32, (1, OWN), 1)
    for j in range(8):
        row = jnp.where(lane < INSIDE, mask_ref[0, j], mask_ref[1, j])
        stats[GROUPS, j : j + 1, :] = row.astype(F32)
    pl.semaphore_wait(barrier, len(peers))

    def send_stats(g):
        for i, peer in zip(SPOTS, around):
            slot = SPOTS.index(8 - i)
            push(STAT + g, stats.at[g], st_ext.at[g, slot], peer)

    def sides(sem, ext, r, b):
        if b == 0:
            push(sem, ext.at[r, 0], ext.at[r, 2], left)
        else:
            push(sem, ext.at[r, 1], ext.at[r, 3], right)

    pieces = [(c // 2, at(c % 2, 32)) for c in range(4)]
    for c, (b, rows) in enumerate(pieces):
        push(N_NEAR + c, n_ext.at[0, b, rows, :], n_ext.at[far, b, rows, :], mate)
    for b in range(2):
        sides(N_MID, n_ext, 0, b)
    push(A2, a2.at[0], a2.at[1], partner)
    send_stats(GROUPS)
    for b in range(2):
        push(G_NEAR + b, g_ext.at[0, b], g_ext.at[far, b], mate)

    def hand_on(c):
        b, rows = pieces[c]
        piece = n_ext.at[near, b, rows, :]
        arrive(N_NEAR + c, piece)
        push(N_FAR + b, piece, n_ext.at[far, b, rows, :], onward)
        if c % 2 == 1:
            sides(N_CORNER, n_ext, near, b)

    def project(rows, targets, first, last):
        def one(j):
            for t, dst in enumerate((q_ext, k_ext, v_ext)):
                part = pl.ds(pl.multiple_of(D * t + GW * j, GW), GW)
                made = dot(rows, w[:, part]).astype(BF16)
                if t == 0:
                    made = made * SCALE
                for i, to in enumerate(targets):
                    dst[to : to + OWN, at(j, GW)] = made[OWN * i : OWN * (i + 1)]

        steps(first, last, one)

    hand_on(0)
    hand_on(1)
    for load in loads:
        load.wait()
    arrive(N_MID, n_ext.at[0, 2:4])
    own_row = n_ext[0].reshape(2 * OWN, D)
    project(own_row, (0, OWN), 0, 2)
    hand_on(2)
    project(own_row, (0, OWN), 2, GROUPS)
    hand_on(3)
    for b in range(2):
        arrive(N_FAR + b, n_ext.at[far, b])
        sides(N_CORNER, n_ext, far, b)
    project(n_ext[1:3, 0:2].reshape(2 * OWN, D), (2 * OWN, 4 * OWN), 0, GROUPS)
    arrive(N_CORNER, n_ext.at[1:3, 2:4])
    project(n_ext[1:3, 2:4].reshape(2 * OWN, D), (3 * OWN, 5 * OWN), 0, GROUPS)
    for b in range(2):
        arrive(G_NEAR + b, g_ext.at[near, b])
        push(G_FAR + b, g_ext.at[near, b], g_ext.at[far, b], onward)
        sides(G_MID, g_ext, 0, b)
        sides(G_CORNER, g_ext, near, b)

    place = lax.broadcasted_iota(jnp.int32, (1, EXT), 1) // INSIDE

    def attend(g):
        cols = at(g, GW)
        k4, v4 = k_ext[:, cols], v_ext[:, cols]
        s_buf[...] = dot_t(spread_heads(q_ext[MINE, cols]), k4)
        dp_buf[...] = dot_t(spread_heads(g_ext[0, 0:2, :, cols].reshape(OWN, GW)), v4)
        bias = []
        for b in range(2):
            allowed = jnp.zeros((1, EXT), jnp.int32)
            for r in range(3):
                for p in range(4):
                    c = COLUMN_OF[p] - b
                    if c < 0 or c > 2:
                        continue
                    m = 3 * ROW_OF[r] + c
                    value = 1 if m == 4 else mask_ref[b, m if m < 4 else m - 1]
                    allowed = jnp.where(place == 4 * r + p, value, allowed)
            bias.append(jnp.where(allowed > 0, 0.0, NEG_BIG))
        lane = lax.broadcasted_iota(jnp.int32, (INSIDE, OWN), 1)
        stat = [jnp.zeros((INSIDE, OWN), F32)] * 2
        for h in range(GROUP):
            for b in range(2):
                part = slice(OWN * h + INSIDE * b, OWN * h + INSIDE * (b + 1))
                s = s_buf[part, :] + bias[b]
                top = jnp.max(s, axis=1, keepdims=True)
                e = jnp.exp(s - top)
                total = jnp.sum(e, axis=1, keepdims=True)
                p = e * (1.0 / total)
                w_buf[part, :] = p.astype(BF16)
                dp = dp_buf[part, :]
                inner = jnp.sum(p * dp, axis=1, keepdims=True)
                ds_buf[part, :] = (p * (dp - inner)).astype(BF16)
                stat[b] = jnp.where(lane == h, top + jnp.log(total), stat[b])
                stat[b] = jnp.where(lane == GROUP + h, inner, stat[b])
        stats[g] = jnp.transpose(jnp.concatenate(stat, axis=0))[0:8]
        send_stats(g)
        mixed = pick_heads(dot(w_buf[...], v4)).astype(BF16).astype(F32)
        dq_all[:, cols] = (pick_heads(dot(ds_buf[...], k4)) * SCALE).astype(BF16)
        out_v[:, :, cols] = (fields_ref[:, :, cols].astype(F32) + tile_of(mixed)).astype(BF16)

    def offer(u, first, second):
        for half in range(2):
            part = slice(HW * half, HW * (half + 1))
            b_own[u, half] = jnp.concatenate([first[:, part], second[:, part]], axis=1)
        push(PAIR + u, b_own.at[u, 1 - core], b_other.at[u], partner)

    def weigh(u):
        arrive(PAIR + u, b_other.at[u])
        both = jnp.concatenate([b_own[u, core], b_other[u]], axis=0)
        for part in range(4):
            rows = slice(256 * part, 256 * (part + 1))
            left_side = jnp.concatenate([a2[0, rows, :], a2[1, rows, :]], axis=1)
            w_send[u, part] = dot(left_side, both).astype(BF16).reshape(4, 2, 32, UW)
        for slot, d in enumerate(SIBLINGS):
            push(ONE + u, w_send.at[u, x_at[d], :, 0], r1.at[u, 0, slot], x_peer[d])
            push(ONE + u, w_send.at[u, :, y_at[d], 1], r1.at[u, 1, slot], y_peer[d])

    def sum_one(u):
        arrive(ONE + u, r1.at[u])
        for i in range(4):
            acc = w_send[u, x, i, 0].astype(F32)
            for slot in range(3):
                acc = acc + r1[u, 0, slot, i].astype(F32)
            s1[u, 0, i] = acc.astype(BF16)
            acc = w_send[u, i, yi, 1].astype(F32)
            for slot in range(3):
                acc = acc + r1[u, 1, slot, i].astype(F32)
            s1[u, 1, i] = acc.astype(BF16)
        for slot, d in enumerate(SIBLINGS):
            push(TWO + u, s1.at[u, 0, y_at[d]], r2.at[u, 0, slot], y_peer[d])
            push(TWO + u, s1.at[u, 1, x_at[d]], r2.at[u, 1, slot], x_peer[d])

    def sum_two(batch):
        for j in range(3):
            u = 3 * batch + j
            arrive(TWO + u, r2.at[u])
            for colour, mine in ((0, yi), (1, x)):
                acc = s1[u, colour, mine].astype(F32)
                for slot in range(3):
                    acc = acc + r2[u, colour, slot].astype(F32)
                for zz in range(4):
                    made = acc[8 * zz : 8 * zz + 8].astype(BF16)
                    s2[batch, 4 * colour + zz, :, UW * j : UW * (j + 1)] = made
        for slot, d in enumerate(FAR_FIRST):
            push(THREE + batch, s2.at[batch, z_at[d]], r3.at[batch, slot], z_peer[d])

    steps(0, 2, attend)
    offer(0, dq_all[:, 0:GW], dq_all[:, GW : 2 * GW])
    for b in range(2):
        arrive(G_FAR + b, g_ext.at[far, b])
        sides(G_CORNER, g_ext, far, b)
    attend(2)
    arrive(A2, a2.at[1])
    weigh(0)
    attend(3)
    offer(1, dq_all[:, 2 * GW : 3 * GW], dq_all[:, 3 * GW :])
    store_out = pltpu.make_async_copy(out_v, out_hbm, local_sem.at[0])
    store_out.start()

    arrive(G_MID, g_ext.at[0, 2:4])
    arrive(G_CORNER, g_ext.at[1:3, 2:4])
    arrive(STAT + GROUPS, st_ext.at[GROUPS])

    def lanes_of(g):
        low = lax.broadcasted_iota(jnp.int32, (8, OWN), 1) < INSIDE

        def spot(i):
            return st_ext[g, SPOTS.index(i)]

        parts = []
        for r in range(3):
            first = 3 * ROW_OF[r]
            parts.append(stats[g] if r == 0 else spot(first + 1))
            parts.append(jnp.where(low, spot(first + 2), spot(first)))
        return jnp.concatenate(parts, axis=1)

    def keys(g):
        cols = at(g, GW)
        arrive(STAT + g, st_ext.at[g])
        q4 = q_ext[:, cols]
        g4 = g_ext[:, :, :, cols].reshape(EXT, GW)
        s_buf[...] = dot_t(spread_heads(k_ext[MINE, cols]), q4)
        dp_buf[...] = dot_t(spread_heads(v_ext[MINE, cols]), g4)
        stat, brick_masks = lanes_of(g), lanes_of(GROUPS)
        bias = []
        for b in range(2):
            allowed = jnp.zeros((1, EXT), F32)
            for r in range(3):
                for p in range(4):
                    c = b + 2 - COLUMN_OF[p]
                    if c < 0 or c > 2:
                        continue
                    m = 3 * (2 - ROW_OF[r]) + c
                    j = m if m < 4 else m - 1
                    value = jnp.ones((1, EXT), F32) if m == 4 else brick_masks[j : j + 1, :]
                    allowed = jnp.where(place == 4 * r + p, value, allowed)
            bias.append(jnp.where(allowed > 0.5, 0.0, NEG_BIG))
        for h in range(GROUP):
            inner = stat[GROUP + h : GROUP + h + 1, :]
            for b in range(2):
                part = slice(OWN * h + INSIDE * b, OWN * h + INSIDE * (b + 1))
                p = jnp.exp(s_buf[part, :] + (bias[b] - stat[h : h + 1, :]))
                w_buf[part, :] = p.astype(BF16)
                ds_buf[part, :] = (p * (dp_buf[part, :] - inner)).astype(BF16)
        dv4 = pick_heads(dot(w_buf[...], g4)).astype(BF16)
        dk4 = pick_heads(dot(ds_buf[...], q4)).astype(BF16)
        dk_all[:, cols] = dk4
        dv_all[:, cols] = dv4
        offer(g + 2, dk4, dv4)
        weigh(g + 1)

        @pl.when(g > 0)
        def _():
            sum_one(g - 1)

    steps(0, GROUPS, keys)
    weigh(GROUPS + 1)

    grads = (dq_all[...], dk_all[...], dv_all[...])
    parts = []
    for j in range(4):
        rows = at(j, GW)
        made = dot_t(grads[0], w[rows, 0:D])
        made = made + dot_t(grads[1], w[rows, D : 2 * D])
        parts.append(made + dot_t(grads[2], w[rows, 2 * D : 3 * D]))
    gn = jnp.concatenate(parts, axis=1)
    xf = bricks_of(fields_ref[...].astype(F32))
    inv = lax.rsqrt(jnp.mean(xf * xf, axis=1, keepdims=True) + EPSILON)
    total = jnp.sum(gn * xf * inv, axis=0, keepdims=True)
    for i in range(8):
        h0[i : i + 1, :] = total[:, 128 * i : 128 * (i + 1)]
    for slot, d in enumerate(SIBLINGS):
        push(GAIN, h0, h1.at[slot], x_peer[d])
    sum_one(3)
    s = gn * gain_ref[...]
    back = inv * (s - xf * inv * inv * jnp.mean(s * xf, axis=1, keepdims=True))
    gin_v[...] = (grad_ref[...].astype(F32) + tile_of(back)).astype(BF16)
    store_gin = pltpu.make_async_copy(gin_v, gin_hbm, local_sem.at[1])
    store_gin.start()

    sum_one(4)
    sum_two(0)
    arrive(GAIN, h1)
    t1[...] = h0[...] + h1[0] + h1[1] + h1[2]
    for slot, d in enumerate(SIBLINGS):
        push(GAIN + 1, t1, h2.at[slot], y_peer[d])
    sum_one(5)
    arrive(GAIN + 1, h2)
    t2[...] = t1[...] + h2[0] + h2[1] + h2[2]
    for slot, d in enumerate(FAR_FIRST):
        push(GAIN + 2, t2, h3.at[slot], z_peer[d])
    sum_two(1)

    arrive(GAIN + 2, h3)
    tot = t2[...]
    for slot in range(7):
        tot = tot + h3[slot]
    t3[...] = tot
    push(GAIN + 3, t3, h4, partner)
    for batch in range(2):
        arrive(THREE + batch, r3.at[batch])
        acc = s2[batch, z].astype(F32)
        for slot in range(7):
            acc = acc + r3[batch, slot].astype(F32)
        acc = acc * (ALL_TOKENS ** (-0.5))
        fin[0, batch] = acc[0:4]
        fin[1, batch] = acc[4:8]
    push(FOUR, fin.at[1 - core], r4, partner)

    for c, (b, rows) in enumerate(pieces):
        leave(N_NEAR + c, n_ext.at[0, b, rows, :])
    for b in range(2):
        leave(N_FAR + b, n_ext.at[0, b])
        leave(G_NEAR + b, g_ext.at[0, b])
        leave(G_FAR + b, g_ext.at[0, b])
    for sem, ext in ((N_MID, n_ext), (G_MID, g_ext)):
        leave(sem, ext.at[0, 2:4])
        leave(sem + 1, ext.at[1:3, 2:4])
    leave(A2, a2.at[0])
    for g in range(GROUPS + 1):
        leave(STAT + g, st_ext.at[g])
    for u in range(UNITS):
        leave(PAIR + u, b_other.at[u])
        leave(ONE + u, r1.at[u])
        leave(TWO + u, r2.at[u])
    for batch in range(2):
        leave(THREE + batch, r3.at[batch])
    for i, ref in enumerate((h1, h2, h3, h4)):
        leave(GAIN + i, ref)
    store_out.wait()
    store_gin.wait()

    arrive(GAIN + 3, h4)
    summed = (t3[...] + h4[...]) * (ALL_TOKENS ** (-0.5))
    t1[...] = summed
    gg_ref[...] = pltpu.roll(t1[pl.ds(gx, 1), :], lax.rem(128 - 4 * gy, 128), 1)
    arrive(FOUR, r4)
    leave(FOUR, r4)
    for batch in range(2):
        mine, other = fin[core, batch], r4[batch]
        is_first = jnp.broadcast_to(core, mine.shape) == 0
        halves = (jnp.where(is_first, mine, other), jnp.where(is_first, other, mine))
        for j in range(3):
            u = 3 * batch + j
            for i in range(2):
                base = GW * (2 * u + i) if u < 2 else D * (1 + i) + GW * (u - 2)
                come = UW * j + HW * i
                for half in range(2):
                    to = base + HW * half
                    wg_ref[:, to : to + HW] = halves[half][:, come : come + HW]


def layer_call(mask, fields, grad_out, gain, w):
    dma = pltpu.SemaphoreType.DMA
    vm = pltpu.VMEM
    tile = (8, 128)
    stack = (GROUP * OWN, EXT)
    return pl.pallas_call(
        layer_kernel,
        out_shape=(
            jax.ShapeDtypeStruct(fields.shape, BF16),
            jax.ShapeDtypeStruct(fields.shape, BF16),
            jax.ShapeDtypeStruct((4, 3 * D), F32),
            jax.ShapeDtypeStruct((1, 128), F32),
        ),
        in_specs=[SM, VM, VM, VM, ANY],
        out_specs=(ANY, ANY, VM, VM),
        scratch_shapes=[
            vm((D, 3 * D), BF16),
            vm((3, 4, INSIDE, D), BF16), vm((3, 4, INSIDE, D), BF16),
            vm((2, D, OWN), BF16),
            vm((EXT, D), BF16), vm((EXT, D), BF16), vm((EXT, D), BF16),
            vm((OWN, D), BF16), vm((OWN, D), BF16), vm((OWN, D), BF16),
            vm(stack, F32), vm(stack, F32), vm(stack, BF16), vm(stack, BF16),
            vm((GROUPS + 1,) + tile, F32), vm((GROUPS + 1, 8) + tile, F32),
            vm(fields.shape, BF16), vm(fields.shape, BF16),
            vm((UNITS, 2, OWN, UW), BF16), vm((UNITS, OWN, UW), BF16),
            vm((UNITS, 4, 4, 2, 32, UW), BF16),
            vm((UNITS, 2, 3, 4, 32, UW), BF16),
            vm((UNITS, 2, 4, 32, UW), BF16),
            vm((UNITS, 2, 3, 32, UW), BF16),
            vm((2, 8, 8, 3 * UW), BF16),
            vm((2, 7, 8, 3 * UW), BF16),
            vm((2, 2, 4, 3 * UW), F32),
            vm((2, 4, 3 * UW), F32),
            vm(tile, F32), vm((3,) + tile, F32),
            vm(tile, F32), vm((3,) + tile, F32),
            vm(tile, F32), vm((7,) + tile, F32),
            vm(tile, F32), vm(tile, F32),
            dma((3,)), dma((SEMS,)), dma((SEMS,)),
        ],
        compiler_params=pltpu.CompilerParams(
            collective_id=0, has_side_effects=True, vmem_limit_bytes=VMEM_LIMIT
        ),
        name="layer",
    )(mask, fields, grad_out, gain, w)


def finish_kernel(out_in, gin_in, wg_in, gg_in, out, gin, wg, gg):
    out[...] = out_in[...]
    gin[...] = gin_in[...]
    wg[...] = wg_in[...]
    for i in range(4):
        gg[i] = gg_in[0, i]


def finish_call(output, grad_in, w_grad, gains):
    return pl.pallas_call(
        finish_kernel,
        out_shape=(
            jax.ShapeDtypeStruct(output.shape, BF16),
            jax.ShapeDtypeStruct(grad_in.shape, BF16),
            jax.ShapeDtypeStruct(w_grad.shape, F32),
            jax.ShapeDtypeStruct((4,), F32),
        ),
        in_specs=[VM] * 4,
        out_specs=(VM, VM, VM, SM),
        name="finish",
    )(output, grad_in, w_grad, gains)


def per_device(fields, grad_out, norm_gain, w_qkv, brick_mask):
    made = layer_call(
        brick_mask.reshape(2, 8), fields, grad_out, norm_gain.reshape(1, D), w_qkv
    )
    return finish_call(*made)


def solution(mesh):
    placed = (P("gx", "gy", None), P("gx", "gy", None), P(), P(), P("gx", "gy", None))
    return jax.shard_map(
        per_device,
        mesh=mesh,
        in_specs=placed,
        out_specs=(
            P("gx", "gy", None),
            P("gx", "gy", None),
            P(("gx", "gy"), None),
            P(("gx", "gy")),
        ),
        check_vma=False,
    )
```

time: 98.5 us -> 74.9 us (0.76)
  Pallas kernels: 91.6 us -> 74.1 us
  local copies, waits for them, and re-layouts: 6.03 us -> 0 us
    pallas_call x1, Pallas kernels: 91.6 us -> 72.3 us  [layer_call(): pl.pallas_call(layer_kernel, out_shape=(jax.ShapeDtypeStruct(fields.shape...]
    unnamed x3 -> x0, local copies, waits for them, and re-layouts: 4.76 us -> none
    pallas_call x0 -> x1, Pallas kernels: none -> 1.86 us  [finish_call(): pl.pallas_call(finish_kernel, out_shape=(jax.ShapeDtypeStruct(output.shap...]
    dynamic_slice x1 -> x0, local copies, waits for them, and re-layouts: 1.27 us -> none  [per_device(): gain_grad = lax.dynamic_slice(gain_sum.reshape(D), (4 * owner,), (4,))]
where the time goes in v3:
time: 74.9 us; the launch traced here: 74.8 us
  Pallas kernels  74.1 us (99%)
    pallas_call x1, Pallas kernels, layer_call(): pl.pallas_call(layer_kernel, out_shape=(jax.ShapeDtypeStruct(fields.shape...  72.3 us
    pallas_call x1, Pallas kernels, finish_call(): pl.pallas_call(finish_kernel, out_shape=(jax.ShapeDtypeStruct(output.shap...  1.86 us

profile of v3, /device:TPU:1, one launch (start us, length us, event | category | flops | bytes accessed | tf_op | source)
XLA Modules:
  0.0 74.8 jit_solution(7376877696159576895)
XLA Ops:
  0.6 72.3 %layer.1 = (bf16[8,16,1024]{2,1,0:T(8,128)(2,1)}, bf16[8,16,1024]{2,1,0:T(8,128)(2,1)}, f32[4,3072]{1,0:T(4,128)}, f32[1,128]{1,0:T(1,128)}) custom-call(s32[2,8]{1,0:T(2,128)} %bitcast.3, bf16[8,16,1024]{2,1,0:T(8,128)(2,1)} %fields_ref.1, bf16[8,16,1024]{2,1,0:T(8,128)(2,1)} %grad_ref.1, f32[1,1024]{1,0:T(1,128)} %bitcast.2, bf16[1024,3072]{1,0:T(8,128)(2,1)} %w_hbm.1), custom_call_target="tpu_custom_call" | custom-call | tf_op jit(solution)/shard_map/layer/pallas_call | solution.py:495
  72.9 1.9 %finish.1 = (bf16[8,16,1024]{2,1,0:T(8,128)(2,1)}, bf16[8,16,1024]{2,1,0:T(8,128)(2,1)}, f32[4,3072]{1,0:T(4,128)}, f32[4]{0:T(128)}) custom-call(bf16[8,16,1024]{2,1,0:T(8,128)(2,1)} %get-tuple-element.8.out_in, bf16[8,16,1024]{2,1,0:T(8,128)(2,1)} %get-tuple-element.9.gin_in, f32[4,3072]{1,0:T(4,128)} %get-tuple-element.10.wg_in, ...), custom_call_target="tpu_custom_call" | custom-call | tf_op jit(solution)/shard_map/finish/pallas_call | solution.py:545

commit v4 on v3

--- a/solution.py
+++ b/solution.py
@@ -94,20 +94,22 @@
 HW = GW // 2
 UNITS = 6
 UW = 2 * HW
+BATCHES = ((1, 2, 3), (4, 5))
 SPOTS = (0, 1, 2, 3, 5, 6, 7, 8)
 MINE = slice(0, OWN)
 SIBLINGS = (2, 1, 3)
 FAR_FIRST = (4, 3, 5, 2, 6, 1, 7)
 (N_NEAR, N_FAR, N_MID, N_CORNER, G_NEAR, G_FAR, G_MID, G_CORNER, A2, STAT, PAIR, ONE, TWO, THREE,
- FOUR, GAIN, SEMS) = (0, 4, 6, 7, 8, 10, 12, 13, 14, 15, 20, 26, 32, 38, 40, 41, 45)
+ FOUR, GAIN, SEMS) = (0, 4, 6, 7, 8, 10, 12, 13, 14, 15, 20, 26, 32, 38, 41, 42, 46)
 
 
 def layer_kernel(
-    mask_ref, fields_ref, grad_ref, gain_ref, w_hbm,
+    mask_ref, fields_hbm, grad_hbm, gain_ref, w_hbm,
     out_hbm, gin_hbm, wg_ref, gg_ref,
-    w, n_ext, g_ext, a2, q_ext, k_ext, v_ext, dq_all, dk_all, dv_all,
+    fields_ref, grad_ref, w, n_ext, g_ext, a2, q_ext, k_ext, v_ext, dq_all, dk_all, dv_all,
     s_buf, dp_buf, w_buf, ds_buf, stats, st_ext, out_v, gin_v,
     b_own, b_other, w_send, r1, s1, r2, s2, r3, fin, r4,
+    z_send, z_r1, z_s1, z_r2, z_s2, z_r3,
     h0, h1, t1, h2, t2, h3, t3, h4,
     local_sem, send, recv,
 ):
@@ -147,6 +149,12 @@
     def leave(i, ref):
         copy_of(i, ref, ref, partner).wait_send()
 
+    tiles = [
+        pltpu.make_async_copy(fields_hbm, fields_ref, local_sem.at[3]),
+        pltpu.make_async_copy(grad_hbm, grad_ref, local_sem.at[4]),
+    ]
+    for load in tiles:
+        load.start()
     loads = [
         pltpu.make_async_copy(w_hbm.at[:, at(t, D)], w.at[:, at(t, D)], local_sem.at[t])
         for t in range(3)
@@ -159,6 +167,8 @@
     for peer in peers:
         pl.semaphore_signal(barrier, inc=1, device_id=peer, device_id_type=MESH)
 
+    for load in tiles:
+        load.wait()
     xf = bricks_of(fields_ref[...].astype(F32))
     inv = lax.rsqrt(jnp.mean(xf * xf, axis=1, keepdims=True) + EPSILON)
     n = (xf * inv * gain_ref[...]).astype(BF16)
@@ -189,8 +199,6 @@
         sides(N_MID, n_ext, 0, b)
     push(A2, a2.at[0], a2.at[1], partner)
     send_stats(GROUPS)
-    for b in range(2):
-        push(G_NEAR + b, g_ext.at[0, b], g_ext.at[far, b], mate)
 
     def hand_on(c):
         b, rows = pieces[c]
@@ -199,6 +207,11 @@
         push(N_FAR + b, piece, n_ext.at[far, b, rows, :], onward)
         if c % 2 == 1:
             sides(N_CORNER, n_ext, near, b)
+
+    def hand_grad_on(b):
+        arrive(G_NEAR + b, g_ext.at[near, b])
+        push(G_FAR + b, g_ext.at[near, b], g_ext.at[far, b], onward)
+        sides(G_CORNER, g_ext, near, b)
 
     def project(rows, targets, first, last):
         def one(j):
@@ -223,16 +236,17 @@
     project(own_row, (0, OWN), 2, GROUPS)
     hand_on(3)
     for b in range(2):
+        push(G_NEAR + b, g_ext.at[0, b], g_ext.at[far, b], mate)
+    for b in range(2):
         arrive(N_FAR + b, n_ext.at[far, b])
         sides(N_CORNER, n_ext, far, b)
+    for b in range(2):
+        sides(G_MID, g_ext, 0, b)
     project(n_ext[1:3, 0:2].reshape(2 * OWN, D), (2 * OWN, 4 * OWN), 0, GROUPS)
+    hand_grad_on(0)
     arrive(N_CORNER, n_ext.at[1:3, 2:4])
     project(n_ext[1:3, 2:4].reshape(2 * OWN, D), (3 * OWN, 5 * OWN), 0, GROUPS)
-    for b in range(2):
-        arrive(G_NEAR + b, g_ext.at[near, b])
-        push(G_FAR + b, g_ext.at[near, b], g_ext.at[far, b], onward)
-        sides(G_MID, g_ext, 0, b)
-        sides(G_CORNER, g_ext, near, b)
+    hand_grad_on(1)
 
     place = lax.broadcasted_iota(jnp.int32, (1, EXT), 1) // INSIDE
 
@@ -292,6 +306,37 @@
             push(ONE + u, w_send.at[u, x_at[d], :, 0], r1.at[u, 0, slot], x_peer[d])
             push(ONE + u, w_send.at[u, :, y_at[d], 1], r1.at[u, 1, slot], y_peer[d])
 
+    def weigh_z():
+        arrive(PAIR, b_other.at[0])
+        both = jnp.concatenate([b_own[0, core], b_other[0]], axis=0)
+        for part in range(4):
+            rows = slice(256 * part, 256 * (part + 1))
+            left_side = jnp.concatenate([a2[0, rows, :], a2[1, rows, :]], axis=1)
+            made = dot(left_side, both)
+            for i in range(32):
+                z_send[i % 8, part, i // 8] = made[8 * i : 8 * i + 8].astype(BF16)
+        for slot, d in enumerate(FAR_FIRST):
+            push(ONE, z_send.at[z_at[d]], z_r1.at[slot], z_peer[d])
+
+    def sum_z_one():
+        arrive(ONE, z_r1)
+        for i in range(4):
+            acc = z_send[z, i].astype(F32)
+            for slot in range(7):
+                acc = acc + z_r1[slot, i].astype(F32)
+            z_s1[i] = acc.astype(BF16)
+        for slot, d in enumerate(SIBLINGS):
+            push(TWO, z_s1.at[x_at[d]], z_r2.at[slot], x_peer[d])
+
+    def sum_z_two():
+        arrive(TWO, z_r2)
+        acc = z_s1[x].astype(F32)
+        for slot in range(3):
+            acc = acc + z_r2[slot].astype(F32)
+        z_s2[...] = acc.astype(BF16)
+        for slot, d in enumerate(SIBLINGS):
+            push(THREE + 2, z_s2.at[y_at[d]], z_r3.at[slot], y_peer[d])
+
     def sum_one(u):
         arrive(ONE + u, r1.at[u])
         for i in range(4):
@@ -308,8 +353,7 @@
             push(TWO + u, s1.at[u, 1, x_at[d]], r2.at[u, 1, slot], x_peer[d])
 
     def sum_two(batch):
-        for j in range(3):
-            u = 3 * batch + j
+        for j, u in enumerate(BATCHES[batch]):
             arrive(TWO + u, r2.at[u])
             for colour, mine in ((0, yi), (1, x)):
                 acc = s1[u, colour, mine].astype(F32)
@@ -318,17 +362,20 @@
                 for zz in range(4):
                     made = acc[8 * zz : 8 * zz + 8].astype(BF16)
                     s2[batch, 4 * colour + zz, :, UW * j : UW * (j + 1)] = made
+        wide = slice(0, UW * len(BATCHES[batch]))
         for slot, d in enumerate(FAR_FIRST):
-            push(THREE + batch, s2.at[batch, z_at[d]], r3.at[batch, slot], z_peer[d])
+            push(
+                THREE + batch, s2.at[batch, z_at[d], :, wide], r3.at[batch, slot, :, wide], z_peer[d]
+            )
 
     steps(0, 2, attend)
     offer(0, dq_all[:, 0:GW], dq_all[:, GW : 2 * GW])
+    attend(2)
+    arrive(A2, a2.at[1])
+    weigh_z()
     for b in range(2):
         arrive(G_FAR + b, g_ext.at[far, b])
         sides(G_CORNER, g_ext, far, b)
-    attend(2)
-    arrive(A2, a2.at[1])
-    weigh(0)
     attend(3)
     offer(1, dq_all[:, 2 * GW : 3 * GW], dq_all[:, 3 * GW :])
     store_out = pltpu.make_async_copy(out_v, out_hbm, local_sem.at[0])
@@ -386,7 +433,7 @@
         offer(g + 2, dk4, dv4)
         weigh(g + 1)
 
-        @pl.when(g > 0)
+        @pl.when(g > 1)
         def _():
             sum_one(g - 1)
 
@@ -415,12 +462,14 @@
     store_gin = pltpu.make_async_copy(gin_v, gin_hbm, local_sem.at[1])
     store_gin.start()
 
+    sum_z_one()
     sum_one(4)
     sum_two(0)
     arrive(GAIN, h1)
     t1[...] = h0[...] + h1[0] + h1[1] + h1[2]
     for slot, d in enumerate(SIBLINGS):
         push(GAIN + 1, t1, h2.at[slot], y_peer[d])
+    sum_z_two()
     sum_one(5)
     arrive(GAIN + 1, h2)
     t2[...] = t1[...] + h2[0] + h2[1] + h2[2]
@@ -434,14 +483,24 @@
         tot = tot + h3[slot]
     t3[...] = tot
     push(GAIN + 3, t3, h4, partner)
-    for batch in range(2):
-        arrive(THREE + batch, r3.at[batch])
-        acc = s2[batch, z].astype(F32)
+
+    def settle(acc, columns):
+        acc = acc * (ALL_TOKENS ** (-0.5))
+        fin[0, :, columns] = acc[0:4]
+        fin[1, :, columns] = acc[4:8]
+
+    arrive(THREE + 2, z_r3)
+    acc = z_s2[yi].astype(F32)
+    for slot in range(3):
+        acc = acc + z_r3[slot].astype(F32)
+    settle(acc, slice(0, UW))
+    for batch, units in enumerate(BATCHES):
+        wide = slice(0, UW * len(units))
+        arrive(THREE + batch, r3.at[batch, :, :, wide])
+        acc = s2[batch, z, :, wide].astype(F32)
         for slot in range(7):
-            acc = acc + r3[batch, slot].astype(F32)
-        acc = acc * (ALL_TOKENS ** (-0.5))
-        fin[0, batch] = acc[0:4]
-        fin[1, batch] = acc[4:8]
+            acc = acc + r3[batch, slot, :, wide].astype(F32)
+        settle(acc, slice(UW * units[0], UW * (units[-1] + 1)))
     push(FOUR, fin.at[1 - core], r4, partner)
 
     for c, (b, rows) in enumerate(pieces):
@@ -458,10 +517,11 @@
         leave(STAT + g, st_ext.at[g])
     for u in range(UNITS):
         leave(PAIR + u, b_other.at[u])
-        leave(ONE + u, r1.at[u])
-        leave(TWO + u, r2.at[u])
-    for batch in range(2):
-        leave(THREE + batch, r3.at[batch])
+        leave(ONE + u, r1.at[u] if u > 0 else z_r1)
+        leave(TWO + u, r2.at[u] if u > 0 else z_r2)
+    for batch, units in enumerate(BATCHES):
+        leave(THREE + batch, r3.at[batch, :, :, 0 : UW * len(units)])
+    leave(THREE + 2, z_r3)
     for i, ref in enumerate((h1, h2, h3, h4)):
         leave(GAIN + i, ref)
     store_out.wait()
@@ -473,18 +533,16 @@
     gg_ref[...] = pltpu.roll(t1[pl.ds(gx, 1), :], lax.rem(128 - 4 * gy, 128), 1)
     arrive(FOUR, r4)
     leave(FOUR, r4)
-    for batch in range(2):
-        mine, other = fin[core, batch], r4[batch]
-        is_first = jnp.broadcast_to(core, mine.shape) == 0
-        halves = (jnp.where(is_first, mine, other), jnp.where(is_first, other, mine))
-        for j in range(3):
-            u = 3 * batch + j
-            for i in range(2):
-                base = GW * (2 * u + i) if u < 2 else D * (1 + i) + GW * (u - 2)
-                come = UW * j + HW * i
-                for half in range(2):
-                    to = base + HW * half
-                    wg_ref[:, to : to + HW] = halves[half][:, come : come + HW]
+    mine, other = fin[core], r4[...]
+    is_first = jnp.broadcast_to(core, mine.shape) == 0
+    halves = (jnp.where(is_first, mine, other), jnp.where(is_first, other, mine))
+    for u in range(UNITS):
+        for i in range(2):
+            base = GW * (2 * u + i) if u < 2 else D * (1 + i) + GW * (u - 2)
+            come = UW * u + HW * i
+            for half in range(2):
+                to = base + HW * half
+                wg_ref[:, to : to + HW] = halves[half][:, come : come + HW]
 
 
 def layer_call(mask, fields, grad_out, gain, w):
@@ -500,9 +558,10 @@
             jax.ShapeDtypeStruct((4, 3 * D), F32),
             jax.ShapeDtypeStruct((1, 128), F32),
         ),
-        in_specs=[SM, VM, VM, VM, ANY],
+        in_specs=[SM, ANY, ANY, VM, ANY],
         out_specs=(ANY, ANY, VM, VM),
         scratch_shapes=[
+            vm(fields.shape, BF16), vm(fields.shape, BF16),
             vm((D, 3 * D), BF16),
             vm((3, 4, INSIDE, D), BF16), vm((3, 4, INSIDE, D), BF16),
             vm((2, D, OWN), BF16),
@@ -518,13 +577,16 @@
             vm((UNITS, 2, 3, 32, UW), BF16),
             vm((2, 8, 8, 3 * UW), BF16),
             vm((2, 7, 8, 3 * UW), BF16),
-            vm((2, 2, 4, 3 * UW), F32),
-            vm((2, 4, 3 * UW), F32),
+            vm((2, 4, UNITS * UW), F32),
+            vm((4, UNITS * UW), F32),
+            vm((8, 4, 4, 8, UW), BF16), vm((7, 4, 4, 8, UW), BF16),
+            vm((4, 4, 8, UW), BF16), vm((3, 4, 8, UW), BF16),
+            vm((4, 8, UW), BF16), vm((3, 8, UW), BF16),
             vm(tile, F32), vm((3,) + tile, F32),
             vm(tile, F32), vm((3,) + tile, F32),
             vm(tile, F32), vm((7,) + tile, F32),
             vm(tile, F32), vm(tile, F32),
-            dma((3,)), dma((SEMS,)), dma((SEMS,)),
+            dma((5,)), dma((SEMS,)), dma((SEMS,)),
         ],
         compiler_params=pltpu.CompilerParams(
             collective_id=0, has_side_effects=True, vmem_limit_bytes=VMEM_LIMIT

time: 74.9 us -> 83.9 us (1.12)
  Pallas kernels: 74.1 us -> 83.2 us
    pallas_call x1, Pallas kernels: 72.3 us -> 81.3 us  [layer_call(): pl.pallas_call(layer_kernel, out_shape=(jax.ShapeDtypeStruct(fields.shape...]
where the time goes in v4:
time: 83.9 us; the launch traced here: 83.8 us
  Pallas kernels  83.2 us (99%)
    pallas_call x1, Pallas kernels, layer_call(): pl.pallas_call(layer_kernel, out_shape=(jax.ShapeDtypeStruct(fields.shape...  81.3 us
    pallas_call x1, Pallas kernels, finish_call(): pl.pallas_call(finish_kernel, out_shape=(jax.ShapeDtypeStruct(output.shap...  1.86 us

profile of v4, /device:TPU:1, one launch (start us, length us, event | category | flops | bytes accessed | tf_op | source)
XLA Modules:
  0.0 83.8 jit_solution(11892664861771867394)
XLA Ops:
  0.6 81.3 %layer.1 = (bf16[8,16,1024]{2,1,0:T(8,128)(2,1)}, bf16[8,16,1024]{2,1,0:T(8,128)(2,1)}, f32[4,3072]{1,0:T(4,128)}, f32[1,128]{1,0:T(1,128)}) custom-call(s32[2,8]{1,0:T(2,128)} %bitcast.3, bf16[8,16,1024]{2,1,0:T(8,128)(2,1)} %fields_hbm.1, bf16[8,16,1024]{2,1,0:T(8,128)(2,1)} %grad_hbm.1, f32[1,1024]{1,0:T(1,128)} %bitcast.2, bf16[1024,3072]{1,0:T(8,128)(2,1)} %w_hbm.1), custom_call_target="tpu_custom_call" | custom-call | tf_op jit(solution)/shard_map/layer/pallas_call | solution.py:553
  82.0 1.9 %finish.1 = (bf16[8,16,1024]{2,1,0:T(8,128)(2,1)}, bf16[8,16,1024]{2,1,0:T(8,128)(2,1)}, f32[4,3072]{1,0:T(4,128)}, f32[4]{0:T(128)}) custom-call(bf16[8,16,1024]{2,1,0:T(8,128)(2,1)} %get-tuple-element.8.out_in, bf16[8,16,1024]{2,1,0:T(8,128)(2,1)} %get-tuple-element.9.gin_in, f32[4,3072]{1,0:T(4,128)} %get-tuple-element.10.wg_in, ...), custom_call_target="tpu_custom_call" | custom-call | tf_op jit(solution)/shard_map/finish/pallas_call | solution.py:607

commit v5 on v3

--- a/solution.py
+++ b/solution.py
@@ -99,7 +99,7 @@
 SIBLINGS = (2, 1, 3)
 FAR_FIRST = (4, 3, 5, 2, 6, 1, 7)
 (N_NEAR, N_FAR, N_MID, N_CORNER, G_NEAR, G_FAR, G_MID, G_CORNER, A2, STAT, PAIR, ONE, TWO, THREE,
- FOUR, GAIN, SEMS) = (0, 4, 6, 7, 8, 10, 12, 13, 14, 15, 20, 26, 32, 38, 40, 41, 45)
+ FOUR, GAIN, HALF, SEMS) = (0, 4, 6, 7, 8, 10, 12, 13, 14, 15, 20, 26, 32, 38, 40, 41, 45, 51)
 
 
 def layer_kernel(
@@ -107,7 +107,7 @@
     out_hbm, gin_hbm, wg_ref, gg_ref,
     w, n_ext, g_ext, a2, q_ext, k_ext, v_ext, dq_all, dk_all, dv_all,
     s_buf, dp_buf, w_buf, ds_buf, stats, st_ext, out_v, gin_v,
-    b_own, b_other, w_send, r1, s1, r2, s2, r3, fin, r4,
+    b_own, b_other, w_send, r1, half, r_half, s1, r2, s2, r3, fin, r4,
     h0, h1, t1, h2, t2, h3, t3, h4,
     local_sem, send, recv,
 ):
@@ -128,6 +128,17 @@
     x_peer = [device(x_at[d], yi, z, core) for d in range(4)]
     y_peer = [device(x, y_at[d], z, core) for d in range(4)]
     z_peer = [device(x, yi, z_at[d], core) for d in range(8)]
+    def trades(c):
+        even_pair, odd_pair = c + 1 - 2 * lax.rem(c, 2), 3 - c
+        return even_pair + core * (odd_pair - even_pair), odd_pair + core * (even_pair - odd_pair)
+
+    def y_index(p):
+        return 2 * lax.rem(p, 2) + p // 2
+
+    fx, sx = trades(x)
+    fy, sy = [y_index(p) for p in trades(2 * (gy // 16) + odd)]
+    ox, oy = 6 - x - fx - sx, 6 - yi - fy - sy
+
     mate = {"gx": gx + 1 - 2 * odd, "gy": gy}
     onward = {"gx": lax.rem(gx + 2 + 4 * odd, 8), "gy": gy}
     near, far = 2 - odd, 1 + odd
@@ -189,8 +200,6 @@
         sides(N_MID, n_ext, 0, b)
     push(A2, a2.at[0], a2.at[1], partner)
     send_stats(GROUPS)
-    for b in range(2):
-        push(G_NEAR + b, g_ext.at[0, b], g_ext.at[far, b], mate)
 
     def hand_on(c):
         b, rows = pieces[c]
@@ -199,6 +208,11 @@
         push(N_FAR + b, piece, n_ext.at[far, b, rows, :], onward)
         if c % 2 == 1:
             sides(N_CORNER, n_ext, near, b)
+
+    def hand_grad_on(b):
+        arrive(G_NEAR + b, g_ext.at[near, b])
+        push(G_FAR + b, g_ext.at[near, b], g_ext.at[far, b], onward)
+        sides(G_CORNER, g_ext, near, b)
 
     def project(rows, targets, first, last):
         def one(j):
@@ -223,16 +237,17 @@
     project(own_row, (0, OWN), 2, GROUPS)
     hand_on(3)
     for b in range(2):
+        push(G_NEAR + b, g_ext.at[0, b], g_ext.at[far, b], mate)
+    for b in range(2):
         arrive(N_FAR + b, n_ext.at[far, b])
         sides(N_CORNER, n_ext, far, b)
+    for b in range(2):
+        sides(G_MID, g_ext, 0, b)
     project(n_ext[1:3, 0:2].reshape(2 * OWN, D), (2 * OWN, 4 * OWN), 0, GROUPS)
+    hand_grad_on(0)
     arrive(N_CORNER, n_ext.at[1:3, 2:4])
     project(n_ext[1:3, 2:4].reshape(2 * OWN, D), (3 * OWN, 5 * OWN), 0, GROUPS)
-    for b in range(2):
-        arrive(G_NEAR + b, g_ext.at[near, b])
-        push(G_FAR + b, g_ext.at[near, b], g_ext.at[far, b], onward)
-        sides(G_MID, g_ext, 0, b)
-        sides(G_CORNER, g_ext, near, b)
+    hand_grad_on(1)
 
     place = lax.broadcasted_iota(jnp.int32, (1, EXT), 1) // INSIDE
 
@@ -288,21 +303,32 @@
             rows = slice(256 * part, 256 * (part + 1))
             left_side = jnp.concatenate([a2[0, rows, :], a2[1, rows, :]], axis=1)
             w_send[u, part] = dot(left_side, both).astype(BF16).reshape(4, 2, 32, UW)
-        for slot, d in enumerate(SIBLINGS):
-            push(ONE + u, w_send.at[u, x_at[d], :, 0], r1.at[u, 0, slot], x_peer[d])
-            push(ONE + u, w_send.at[u, :, y_at[d], 1], r1.at[u, 1, slot], y_peer[d])
+        for slot, to in enumerate((ox, fx)):
+            push(ONE + u, w_send.at[u, to, :, 0], r1.at[u, 0, slot], device(fx, yi, z, core))
+        for slot, to in enumerate((oy, fy)):
+            push(ONE + u, w_send.at[u, :, to, 1], r1.at[u, 1, slot], device(x, fy, z, core))
+
+    def sum_half(u):
+        arrive(ONE + u, r1.at[u])
+
+        def one(i):
+            half[u, 0, i] = (w_send[u, sx, i, 0].astype(F32) + r1[u, 0, 0, i].astype(F32)).astype(BF16)
+            half[u, 1, i] = (w_send[u, i, sy, 1].astype(F32) + r1[u, 1, 0, i].astype(F32)).astype(BF16)
+
+        steps(0, 4, one)
+        push(HALF + u, half.at[u, 0], r_half.at[u, 0], device(sx, yi, z, core))
+        push(HALF + u, half.at[u, 1], r_half.at[u, 1], device(x, sy, z, core))
 
     def sum_one(u):
-        arrive(ONE + u, r1.at[u])
-        for i in range(4):
-            acc = w_send[u, x, i, 0].astype(F32)
-            for slot in range(3):
-                acc = acc + r1[u, 0, slot, i].astype(F32)
-            s1[u, 0, i] = acc.astype(BF16)
-            acc = w_send[u, i, yi, 1].astype(F32)
-            for slot in range(3):
-                acc = acc + r1[u, 1, slot, i].astype(F32)
-            s1[u, 1, i] = acc.astype(BF16)
+        arrive(HALF + u, r_half.at[u])
+
+        def one(i):
+            acc = w_send[u, x, i, 0].astype(F32) + r1[u, 0, 1, i].astype(F32)
+            s1[u, 0, i] = (acc + r_half[u, 0, i].astype(F32)).astype(BF16)
+            acc = w_send[u, i, yi, 1].astype(F32) + r1[u, 1, 1, i].astype(F32)
+            s1[u, 1, i] = (acc + r_half[u, 1, i].astype(F32)).astype(BF16)
+
+        steps(0, 4, one)
         for slot, d in enumerate(SIBLINGS):
             push(TWO + u, s1.at[u, 0, y_at[d]], r2.at[u, 0, slot], y_peer[d])
             push(TWO + u, s1.at[u, 1, x_at[d]], r2.at[u, 1, slot], x_peer[d])
@@ -321,16 +347,26 @@
         for slot, d in enumerate(FAR_FIRST):
             push(THREE + batch, s2.at[batch, z_at[d]], r3.at[batch, slot], z_peer[d])
 
-    steps(0, 2, attend)
-    offer(0, dq_all[:, 0:GW], dq_all[:, GW : 2 * GW])
-    for b in range(2):
-        arrive(G_FAR + b, g_ext.at[far, b])
-        sides(G_CORNER, g_ext, far, b)
-    attend(2)
-    arrive(A2, a2.at[1])
-    weigh(0)
-    attend(3)
-    offer(1, dq_all[:, 2 * GW : 3 * GW], dq_all[:, 3 * GW :])
+    def forward(g):
+        attend(g)
+
+        @pl.when(g == 1)
+        def _():
+            offer(0, dq_all[:, 0:GW], dq_all[:, GW : 2 * GW])
+
+        @pl.when(g == 2)
+        def _():
+            for b in range(2):
+                arrive(G_FAR + b, g_ext.at[far, b])
+                sides(G_CORNER, g_ext, far, b)
+            arrive(A2, a2.at[1])
+            weigh(0)
+
+        @pl.when(g == 3)
+        def _():
+            offer(1, dq_all[:, 2 * GW : 3 * GW], dq_all[:, 3 * GW :])
+
+    steps(0, GROUPS, forward)
     store_out = pltpu.make_async_copy(out_v, out_hbm, local_sem.at[0])
     store_out.start()
 
@@ -385,6 +421,7 @@
         dv_all[:, cols] = dv4
         offer(g + 2, dk4, dv4)
         weigh(g + 1)
+        sum_half(g)
 
         @pl.when(g > 0)
         def _():
@@ -408,6 +445,7 @@
         h0[i : i + 1, :] = total[:, 128 * i : 128 * (i + 1)]
     for slot, d in enumerate(SIBLINGS):
         push(GAIN, h0, h1.at[slot], x_peer[d])
+    sum_half(4)
     sum_one(3)
     s = gn * gain_ref[...]
     back = inv * (s - xf * inv * inv * jnp.mean(s * xf, axis=1, keepdims=True))
@@ -415,6 +453,7 @@
     store_gin = pltpu.make_async_copy(gin_v, gin_hbm, local_sem.at[1])
     store_gin.start()
 
+    sum_half(5)
     sum_one(4)
     sum_two(0)
     arrive(GAIN, h1)
@@ -459,6 +498,7 @@
     for u in range(UNITS):
         leave(PAIR + u, b_other.at[u])
         leave(ONE + u, r1.at[u])
+        leave(HALF + u, r_half.at[u])
         leave(TWO + u, r2.at[u])
     for batch in range(2):
         leave(THREE + batch, r3.at[batch])
@@ -513,7 +553,9 @@
             vm(fields.shape, BF16), vm(fields.shape, BF16),
             vm((UNITS, 2, OWN, UW), BF16), vm((UNITS, OWN, UW), BF16),
             vm((UNITS, 4, 4, 2, 32, UW), BF16),
-            vm((UNITS, 2, 3, 4, 32, UW), BF16),
+            vm((UNITS, 2, 2, 4, 32, UW), BF16),
+            vm((UNITS, 2, 4, 32, UW), BF16),
+            vm((UNITS, 2, 4, 32, UW), BF16),
             vm((UNITS, 2, 4, 32, UW), BF16),
             vm((UNITS, 2, 3, 32, UW), BF16),
             vm((2, 8, 8, 3 * UW), BF16),

time: 74.9 us -> 76.7 us (1.024)
  Pallas kernels: 74.1 us -> 75.9 us
    pallas_call x1, Pallas kernels: 72.3 us -> 74.1 us  [layer_call(): pl.pallas_call(layer_kernel, out_shape=(jax.ShapeDtypeStruct(fields.shape...]
where the time goes in v5:
time: 76.7 us; the launch traced here: 76.6 us
  Pallas kernels  75.9 us (99%)
    pallas_call x1, Pallas kernels, layer_call(): pl.pallas_call(layer_kernel, out_shape=(jax.ShapeDtypeStruct(fields.shape...  74.1 us
    pallas_call x1, Pallas kernels, finish_call(): pl.pallas_call(finish_kernel, out_shape=(jax.ShapeDtypeStruct(output.shap...  1.86 us

profile of v5, /device:TPU:1, one launch (start us, length us, event | category | flops | bytes accessed | tf_op | source)
XLA Modules:
  0.0 76.6 jit_solution(6006637305658403837)
XLA Ops:
  0.6 74.1 %layer.1 = (bf16[8,16,1024]{2,1,0:T(8,128)(2,1)}, bf16[8,16,1024]{2,1,0:T(8,128)(2,1)}, f32[4,3072]{1,0:T(4,128)}, f32[1,128]{1,0:T(1,128)}) custom-call(s32[2,8]{1,0:T(2,128)} %bitcast.3, bf16[8,16,1024]{2,1,0:T(8,128)(2,1)} %fields_ref.1, bf16[8,16,1024]{2,1,0:T(8,128)(2,1)} %grad_ref.1, f32[1,1024]{1,0:T(1,128)} %bitcast.2, bf16[1024,3072]{1,0:T(8,128)(2,1)} %w_hbm.1), custom_call_target="tpu_custom_call" | custom-call | tf_op jit(solution)/shard_map/layer/pallas_call | solution.py:535
  74.7 1.9 %finish.1 = (bf16[8,16,1024]{2,1,0:T(8,128)(2,1)}, bf16[8,16,1024]{2,1,0:T(8,128)(2,1)}, f32[4,3072]{1,0:T(4,128)}, f32[4]{0:T(128)}) custom-call(bf16[8,16,1024]{2,1,0:T(8,128)(2,1)} %get-tuple-element.8.out_in, bf16[8,16,1024]{2,1,0:T(8,128)(2,1)} %get-tuple-element.9.gin_in, f32[4,3072]{1,0:T(4,128)} %get-tuple-element.10.wg_in, ...), custom_call_target="tpu_custom_call" | custom-call | tf_op jit(solution)/shard_map/finish/pallas_call | solution.py:587
